TPU v7x, 1024 devices: a whole 4x4x32 slice. The times are simulated.
1024 devices in a mesh: row: 64 (over z, core), vec: 16 (over y, x).
Axes of the slice: x: 4, y: 4, z: 32, core: 2. Of those that a mesh axis runs over, the one named last changes fastest.
Arguments:
- vectors: float32 [131072, 2048], P('row', 'vec'), may hold values from -6 to 6
- band_head: float32 [128, 131072], P(None, 'row'), may hold values from -0.125 to 0.125
- band_tail: float32 [128, 32768], P(None, 'row'), may hold values from -0.125 to 0.125
- band_factor: float32 [64, 128, 128], P('row'), may hold values from -0.5 to 0.5
- panel_vectors: bfloat16 [2, 512, 131072], P(None, 'vec', 'row'), may hold values from -0.03125 to 0.03125
- panel_factor: float32 [2, 512, 512], replicated, may hold values from -0.25 to 0.25
Outputs:
- result: float32 [131072, 2048], P('row', 'vec')
All inputs are finite; a program needn't handle non-finite values.
Results may differ from a plain program's by a relative error of at most 0.0003.
Values may be sent and summed in bfloat16 or wider, within the bound.
No kernel may reach another device: no remote copies, remote signals or barrier semaphores. Data moves between devices by JAX's collectives and lax.ppermute only.
A program may use at most 64 MiB of HBM per device.

v0:
```python
import functools

import jax
import jax.numpy as jnp
from jax import lax
from jax.sharding import Mesh
from jax.sharding import PartitionSpec as P

ROW = ("row_0", "row_1")


HIGHEST = lax.Precision.HIGHEST


def from_behind(array, axis, by):
    devices = lax.axis_size(axis)
    return lax.ppermute(array, axis, [(i, (i + by) % devices) for i in range(devices)])


def laid_out(pieces, dim):
    pieces = jnp.moveaxis(pieces, 0, dim)
    dims = pieces.shape
    return pieces.reshape(*dims[:dim], dims[dim] * dims[dim + 1], *dims[dim + 2 :])


def from_everyone(array, axis):
    copies = jnp.broadcast_to(array, (lax.axis_size(axis), *array.shape))
    return lax.all_to_all(copies, axis, split_axis=0, concat_axis=0, tiled=True)


def collect(array, axis, dim):
    return laid_out(from_everyone(array, axis), dim)


def one_axis_at_a_time(array, axes):
    return functools.reduce(lax.psum, axes, array)


def product(left, right):
    return jnp.dot(left, right, precision=HIGHEST, preferred_element_type=jnp.float32)


def on_device(vectors, band_head, band_tail, band_factor, panel_vectors, panel_factor):
    margin_rows = band_tail.shape[1]
    parity = lax.axis_index(ROW) % 2
    factor = jnp.triu(band_factor[0])
    current = vectors
    for sweep_phase in range(2):
        active = parity == sweep_phase
        own_part = product(band_head, current)
        tail_part = product(band_tail, current[:margin_rows])
        from_next = from_behind(tail_part, ROW, -1)
        weights = product(factor, own_part + from_next)
        from_prev = from_behind(weights, ROW, 1)
        owned_rows = current - product(band_head.T, weights)
        top_new = current[:margin_rows] - product(band_tail.T, from_prev)
        current = jnp.where(
            active, owned_rows, jnp.concatenate([top_new, current[margin_rows:]], axis=0)
        )
    panel_tri = jnp.triu(panel_factor)
    for panel_index in range(panel_vectors.shape[0]):
        panel_rows = collect(panel_vectors[panel_index], "vec", 0)
        panel_wide = panel_rows.astype(jnp.float32)
        partial_value = product(panel_wide, current)
        summed = one_axis_at_a_time(partial_value, ROW)
        weights = product(panel_tri[panel_index], summed)
        current = current - product(panel_wide.T, weights)
    return current


def solution(mesh):
    split = Mesh(mesh.devices.reshape(32, 2, mesh.shape["vec"]), ("row_0", "row_1", "vec"))
    return jax.shard_map(
        on_device,
        mesh=split,
        in_specs=(
            P(ROW, "vec"),
            P(None, ROW),
            P(None, ROW),
            P(ROW, None, None),
            P(None, "vec", ROW),
            P(),
        ),
        out_specs=P(ROW, "vec"),
        check_vma=False,
    )
```

profile of v0, /device:TPU:1, one launch (start us, length us, event | category | flops | bytes accessed | tf_op | source)
XLA Modules:
  0.0 743.5 jit_solution(2409048248850122275)
XLA Ops:
  6.5 1.7 copy.8
  9.2 14.1 %collective-permute-start = (f32[128,128]{1,0:T(8,128)}, f32[128,128]{1,0:T(8,128)}, u32[]{:S(2)}, u32[]{:S(2)}) collective-permute-start(f32[128,128]{1,0:T(8,128)} %fusion.10), channel_id=1, source_target_pairs={{0,1008},{16,0},{32,16},{48,32},{64,48},{80,64},{96,80},{112,96},{... | collective-permute-start | bytes 196616 | tf_op jit(solution)/shard_map/ppermute | solution.py:17
  23.4 1.6 broadcast_in_dim.21
  25.0 4.6 all-to-all-start
  29.6 2.0 convolution_add_fusion
  32.8 6.0 collective-permute-done.1
  39.3 2.3 maximum_select_fusion
  41.9 4.2 collective-permute-start.2
  49.0 4.3 all-to-all-done
  53.3 1.6 broadcast_in_dim.22
  54.9 5.1 all-to-all-start.1
  60.1 2.0 fusion.3
  64.1 4.5 convolution_bitcast_fusion.5
  68.8 252.2 %all-reduce.5.cloned.1.call-done = f32[512,128]{0,1:T(8,128)} async-done(((f32[512,128]{0,1:T(8,128)}), f32[512,128]{0,1:T(8,128)}) %all-reduce.5.cloned.1.call-update) | async-done | bytes 262160 | tf_op jit(solution)/shard_map/psum | solution.py:36
  321.3 3.3 broadcast_select_fusion
  324.7 74.3 %all-reduce.7.cloned.1.call-done = f32[512,128]{0,1:T(8,128)} async-done(((f32[512,128]{0,1:T(8,128)}), f32[512,128]{0,1:T(8,128)}) %all-reduce.7.cloned.1.call-update) | async-done | bytes 262160 | tf_op jit(solution)/shard_map/psum | solution.py:36
  399.0 2.3 fusion.8
  401.2 2.9 fusion.1
  404.1 4.5 convolution_bitcast_fusion.4
  408.6 244.4 %all-reduce.9.cloned.1.call-done = f32[512,128]{0,1:T(8,128)} async-done(((f32[512,128]{0,1:T(8,128)}), f32[512,128]{0,1:T(8,128)}) %all-reduce.9.cloned.1.call-update) | async-done | bytes 262160 | tf_op jit(solution)/shard_map/psum | solution.py:36
  653.1 77.7 %all-reduce.11.cloned.1.call-done = f32[512,128]{0,1:T(8,128)} async-done(((f32[512,128]{0,1:T(8,128)}), f32[512,128]{0,1:T(8,128)}) %all-reduce.11.cloned.1.call-update) | async-done | bytes 262160 | tf_op jit(solution)/shard_map/psum | solution.py:36
  730.8 2.3 fusion.7
  733.0 2.7 fusion
  735.7 1.3 copy.10
  (47 shorter events, 8.6 us)
Async XLA Ops:
  6.5 23.0 %copy-start = (f32[128,2048]{1,0:T(8,128)S(1)}, f32[128,2048]{1,0:T(8,128)}, u32[]{:S(2)}) copy-start(f32[128,2048]{1,0:T(8,128)} %param.7) | copy-start | bytes 3145732
  6.5 1.7 copy-start.3
  6.5 16.8 %copy-start.9 = (bf16[2,32,2048]{2,1,0:T(8,128)(2,1)S(1)}, bf16[2,32,2048]{2,1,0:T(8,128)(2,1)}, u32[]{:S(2)}) copy-start(bf16[2,32,2048]{2,1,0:T(8,128)(2,1)} %param.10) | copy-start | bytes 786436
  9.2 20.3 %collective-permute-start = (f32[128,128]{1,0:T(8,128)}, f32[128,128]{1,0:T(8,128)}, u32[]{:S(2)}, u32[]{:S(2)}) collective-permute-start(f32[128,128]{1,0:T(8,128)} %fusion.10), channel_id=1, source_target_pairs={{0,1008},{16,0},{32,16},{48,32},{64,48},{80,64},{96,80},{112,96},{... | collective-permute-start | bytes 196616 | tf_op jit(solution)/shard_map/ppermute | solution.py:17
  24.9 4.6 copy-start.2
  25.0 28.3 %all-to-all-start = ((bf16[16,32,2048]{2,1,0:T(8,128)(2,1)}), bf16[16,32,2048]{2,1,0:T(8,128)(2,1)}, u32[]{:S(2)}, u32[]{:S(2)}) async-start(bf16[16,32,2048]{2,1,0:T(8,128)(2,1)} %broadcast_in_dim.21), calls=%async_computation | async-start | bytes 4194304 | tf_op jit(solution)/shard_map/all_to_all | solution.py:28
  29.5 2.0 copy-start.7
  31.8 7.0 copy-start.6
  31.9 7.0 collective-permute-start.1
  41.5 6.5 copy-start.8
  41.9 5.1 collective-permute-start.2
  49.0 13.1 %collective-permute-start.3 = (f32[128,128]{1,0:T(8,128)}, f32[128,128]{1,0:T(8,128)}, u32[]{:S(2)}, u32[]{:S(2)}) collective-permute-start(f32[128,128]{1,0:T(8,128)} %fusion.12), channel_id=1, source_target_pairs={{0,16},{16,32},{32,48},{48,64},{64,80},{80,96},{96,112},{112,128},... | collective-permute-start | bytes 196616 | tf_op jit(solution)/shard_map/ppermute | solution.py:17
  54.9 349.2 %all-to-all-start.1 = ((bf16[16,32,2048]{2,1,0:T(8,128)(2,1)}), bf16[16,32,2048]{2,1,0:T(8,128)(2,1)}, u32[]{:S(2)}, u32[]{:S(2)}) async-start(bf16[16,32,2048]{2,1,0:T(8,128)(2,1)} %broadcast_in_dim.22), calls=%async_computation.1 | async-start | bytes 4194304 | tf_op jit(solution)/shard_map/all_to_all | solution.py:28
  60.0 261.0 %all-reduce.5.cloned.1.call-start = ((), (), s32[]{:S(2)}) async-start(), calls=%async_computation.2 | async-start | bytes 524288 | tf_op jit(solution)/shard_map/psum | solution.py:36
  60.1 4.0 copy-start.1
  63.3 0.7 copy-start.4
  68.6 330.4 %all-reduce.7.cloned.1.call-start = ((), (), s32[]{:S(2)}) async-start(), calls=%async_computation.3 | async-start | bytes 524288 | tf_op jit(solution)/shard_map/psum | solution.py:36
  321.1 80.1 %copy-start.5 = (f32[512,128]{0,1:T(8,128)S(1)}, f32[512,128]{0,1:T(8,128)}, u32[]{:S(2)}) copy-start(f32[512,128]{0,1:T(8,128)} %copy-done.4) | copy-start | bytes 786436
  321.1 331.9 %all-reduce.9.cloned.1.call-start = ((), (), s32[]{:S(2)}) async-start(), calls=%async_computation.4 | async-start | bytes 524288 | tf_op jit(solution)/shard_map/psum | solution.py:36
  408.6 322.2 %all-reduce.11.cloned.1.call-start = ((), (), s32[]{:S(2)}) async-start(), calls=%async_computation.5 | async-start | bytes 524288 | tf_op jit(solution)/shard_map/psum | solution.py:36
Sparse Core Ops, SparseCore 0:
  68.7 252.3 all-reduce.4
  324.5 74.3 all-reduce.6
  408.7 244.2 all-reduce.8
  656.3 74.3 all-reduce.10
where the time goes:
time: 744 us
  waiting for transfers between devices  659 us (89%)
  matrix products  30.4 us (4%)
  starting transfers between devices  28.4 us (4%)
  between operations  13.4 us (2%)
  local copies, waits for them, and re-layouts  8.82 us (1%)
    psum x4, waiting for transfers between devices, one_axis_at_a_time(): return functools.reduce(lax.psum, axes, array)  649 us
    dot_general x16, matrix products, product(): jnp.dot(left, right, precision=HIGHEST, preferred_element_type=jnp.float32)  30.4 us
    ppermute x4, starting transfers between devices, from_behind(): lax.ppermute(array, axis, [(i, (i + by) % devices) for i in range(devices)])  18.3 us
  transfers between devices with their start and end apart: 10, of which 6 were waited for; matrix products, arithmetic and copies ran while one was open for 4% of the time, Pallas kernels for 0%

commit v1 on v0

v1 whole, which is shorter than its diff:
```python
import jax
import jax.numpy as jnp
from jax import lax
from jax.sharding import Mesh
from jax.sharding import PartitionSpec as P

ROW = ("far", "near", "core")
NEAR = ("near", "core")
CHIPS = ("far", "near")
HIGHEST = lax.Precision.HIGHEST
F32 = jnp.float32
BF16 = jnp.bfloat16


def product(left, right):
    return jnp.dot(left, right, precision=HIGHEST, preferred_element_type=F32)


def product_t(left, right):
    return lax.dot_general(left, right, (((0,), (0,)), ((), ())), precision=HIGHEST, preferred_element_type=F32)


def product_nt(left, right):
    return lax.dot_general(left, right, (((1,), (1,)), ((), ())), precision=HIGHEST, preferred_element_type=F32)


def thirds(array):
    high = lax.reduce_precision(array, 8, 7)
    rest = array - high
    mid = lax.reduce_precision(rest, 8, 7)
    low = rest - mid
    return jnp.concatenate([high.astype(BF16), mid.astype(BF16), low.astype(BF16)], axis=1)


def fold(wide):
    width = wide.shape[1] // 3
    return wide[:, :width] + (wide[:, width : 2 * width] + wide[:, 2 * width :])


def to_everyone(array, axis):
    copies = jnp.broadcast_to(array, (lax.axis_size(axis), *array.shape))
    return lax.all_to_all(copies, axis, split_axis=0, concat_axis=0, tiled=True)


def swapped(array):
    return lax.ppermute(array, "core", [(0, 1), (1, 0)])


def halves(array):
    middle = array.shape[0] // 2
    return array[:middle], array[middle:]


def core_share(partial, first):
    low, high = halves(partial)
    return jnp.where(first, low, high) + swapped(jnp.where(first, high, low))


def joined(mine, other, first):
    return jnp.concatenate([jnp.where(first, mine, other), jnp.where(first, other, mine)], axis=0)


def summed_over_rows(part_a, part_b, first):
    group = lax.axis_size("near")
    width = part_a.shape[1]
    share_a, share_b = core_share(part_a, first), core_share(part_b, first)
    cut = share_a.shape[0] // group
    blocks = jnp.concatenate([share_a.reshape(group, -1, width), share_b.reshape(group, -1, width)], axis=1)
    share = jnp.sum(lax.all_to_all(blocks, "near", split_axis=0, concat_axis=0, tiled=True), axis=0)
    share = jnp.sum(to_everyone(share, "far"), axis=0)
    mine = to_everyone(share, "near")
    other = swapped(mine)
    sum_a = joined(mine[:, :cut].reshape(-1, width), other[:, :cut].reshape(-1, width), first)
    sum_b = joined(mine[:, cut:].reshape(-1, width), other[:, cut:].reshape(-1, width), first)
    return sum_a, sum_b


def on_device(vectors, band_head, band_tail, band_factor, panel_vectors, panel_factor):
    margin = band_tail.shape[1]
    own_chunk, width = panel_vectors.shape[1], vectors.shape[1]
    depth = panel_factor.shape[1]
    even = lax.axis_index("core") == 0
    n = lax.axis_size(ROW)

    panel0 = to_everyone(panel_vectors[0], "vec").reshape(depth, -1)
    panel1 = to_everyone(panel_vectors[1], "vec").reshape(depth, -1)

    factor = jnp.triu(band_factor[0])
    own = product(band_head, vectors)
    tail = product(band_tail, vectors[:margin])
    cross = product_nt(band_tail, band_head[:, :margin])
    tail_next = lax.ppermute(tail, ROW, [(i + 1, i) for i in range(0, n, 2)])
    weights_a = product(factor, own + tail_next)
    weights_a_prev = lax.ppermute(weights_a, ROW, [(i, i + 1) for i in range(0, n, 2)])
    tail_b = tail - product(cross, weights_a)
    tail_b_next = lax.ppermute(tail_b, ROW, [(i, (i - 1) % n) for i in range(0, n, 2)])
    weights_b = product(factor, own - product_t(cross, weights_a_prev) + tail_b_next)
    weights_b_prev = lax.ppermute(weights_b, ROW, [(i, (i + 1) % n) for i in range(1, n, 2)])
    weights_own = jnp.where(even, weights_a, weights_b)
    weights_prev = jnp.where(even, weights_b_prev, weights_a_prev)
    current = vectors - product_t(band_head, weights_own)
    top = current[:margin] - product_t(band_tail, weights_prev)
    current = jnp.concatenate([top, current[margin:]], axis=0)

    split = thirds(current)
    part0 = fold(jnp.dot(panel0, split, preferred_element_type=F32))
    gram = lax.dot_general(panel_vectors[1], panel0, (((1,), (1,)), ((), ())), preferred_element_type=F32)
    pieces = depth // width
    gram_rows = jnp.concatenate([gram[:, i * width : (i + 1) * width] for i in range(pieces)], axis=0)
    mixed = jnp.concatenate(
        [part0[: depth // 2], gram_rows[: width // 2], part0[depth // 2 :], gram_rows[width // 2 :]], axis=0
    )
    part1 = fold(jnp.dot(panel1, split, preferred_element_type=F32))
    mixed_sum, sum1 = summed_over_rows(mixed, part1, even)
    low, high = halves(mixed_sum)
    sum0 = jnp.concatenate([low[: depth // 2], high[: depth // 2], low[depth // 2 :], high[depth // 2 :]], axis=0)

    gram_own = jnp.concatenate([sum0[depth + i * own_chunk : depth + (i + 1) * own_chunk] for i in range(pieces)], axis=1)
    gram_all = to_everyone(gram_own, "vec").reshape(depth, depth)
    tri = jnp.triu(panel_factor)
    w0 = product(tri[0], sum0[:depth])
    w1 = product(tri[1], sum1 - product(gram_all, w0))

    def spread(panel, w):
        return fold(lax.dot_general(panel, thirds(w), (((0,), (0,)), ((), ())), preferred_element_type=F32))

    return current - spread(panel0, w0) - spread(panel1, w1)


def solution(mesh):
    devices = mesh.devices.reshape(4, 8, 2, mesh.shape["vec"])
    split = Mesh(devices, ("far", "near", "core", "vec"))
    return jax.shard_map(
        on_device,
        mesh=split,
        in_specs=(
            P(ROW, "vec"),
            P(None, ROW),
            P(None, ROW),
            P(ROW, None, None),
            P(None, "vec", ROW),
            P(),
        ),
        out_specs=P(ROW, "vec"),
        check_vma=False,
    )
```

time: 744 us -> 240 us (0.32)
  waiting for transfers between devices: 659 us -> 9.87 us
  blocking collectives: 0 us -> 101 us
  starting transfers between devices: 28.4 us -> 68.5 us
  between operations: 13.4 us -> 0.56 us
  other arithmetic: 3.53 us -> 11.9 us
    psum x4 -> x0, waiting for transfers between devices: 649 us -> none  [one_axis_at_a_time(): return functools.reduce(lax.psum, axes, array)]
    all_to_all x0 -> x3, blocking collectives: none -> 101 us  [the longest x2 67.1 us: to_everyone(): return lax.all_to_all(copies, axis, split_axis=0, concat_axis=0, tiled=True)]
    ppermute x4 -> x7, starting transfers between devices: 18.3 us -> 50.8 us  [the longest x3 23.9 us: swapped(): return lax.ppermute(array, 'core', [(0, 1), (1, 0)])]
    all_to_all x2 -> x3, starting transfers between devices: 9.72 us -> 17.6 us  [to_everyone(): return lax.all_to_all(copies, axis, split_axis=0, concat_axis=0, tiled=True)]
    dot_general x16 -> x17, matrix products: 30.4 us -> 31.3 us  [the longest x8 13.1 us: product(): return jnp.dot(left, right, precision=HIGHEST, preferred_element_type=F32)]
  transfers between devices with their start and end apart: 10 -> 10, of which waited for: 6 -> 3; matrix products, arithmetic and copies ran while one was open for 4% -> 14% of each run, Pallas kernels for 0% -> 0%
where the time goes in v1:
time: 240 us; the launch traced here: 238 us
  blocking collectives  101 us (42%)
  starting transfers between devices  68.5 us (29%)
  matrix products  31.3 us (13%)
  local copies, waits for them, and re-layouts  15.3 us (6%)
  other arithmetic  11.9 us (5%)
  waiting for transfers between devices  9.87 us (4%)
    all_to_all x2, blocking collectives, to_everyone(): return lax.all_to_all(copies, axis, split_axis=0, concat_axis=0, tiled=True)  67.1 us
    all_to_all x1, blocking collectives, summed_over_rows(): lax.all_to_all(blocks, 'near', split_axis=0, concat_axis=0, tiled=True)  34 us
    ppermute x3, starting transfers between devices, swapped(): return lax.ppermute(array, 'core', [(0, 1), (1, 0)])  23.9 us
    all_to_all x3, starting transfers between devices, to_everyone(): return lax.all_to_all(copies, axis, split_axis=0, concat_axis=0, tiled=True)  17.6 us
    dot_general x8, matrix products, product(): return jnp.dot(left, right, precision=HIGHEST, preferred_element_type=F32)  13.1 us
    ppermute x1, starting transfers between devices, on_device(): lax.ppermute(weights_b, ROW, [(i, (i + 1) % n) for i in range(1, n, 2)])  12.2 us
    ppermute x1, starting transfers between devices, on_device(): tail_next = lax.ppermute(tail, ROW, [(i + 1, i) for i in range(0, n, 2)])  12.2 us
    all_to_all x3, waiting for transfers between devices, to_everyone(): return lax.all_to_all(copies, axis, split_axis=0, concat_axis=0, tiled=True)  9.59 us
  transfers between devices with their start and end apart: 10, of which 3 were waited for; matrix products, arithmetic and copies ran while one was open for 14% of the time, Pallas kernels for 0%

profile of v1, /device:TPU:1, one launch (start us, length us, event | category | flops | bytes accessed | tf_op | source)
XLA Modules:
  0.0 238.5 jit_solution(953166746925952949)
XLA Ops:
  3.3 7.7 %all-to-all-start = ((bf16[16,32,2048]{2,1,0:T(8,128)(2,1)}), bf16[16,32,2048]{2,1,0:T(8,128)(2,1)S(1)}, u32[]{:S(2)}, u32[]{:S(2)}) async-start(bf16[16,32,2048]{2,1,0:T(8,128)(2,1)} %broadcast_in_dim.30), calls=%async_computation | async-start | bytes 4194304 | tf_op jit(solution)/shard_map/all_to_all | solution.py:42
  11.4 12.2 %collective-permute-start = (f32[128,128]{1,0:T(8,128)S(1)}, f32[128,128]{1,0:T(8,128)S(1)}, u32[]{:S(2)}, u32[]{:S(2)}) collective-permute-start(f32[128,128]{1,0:T(8,128)S(1)} %fusion.31), channel_id=1, source_target_pairs={{16,0},{48,32},{80,64},{112,96},{144,128},{176,160},{208,192},{240... | collective-permute-start | bytes 196616 | tf_op jit(solution)/shard_map/ppermute | solution.py:92
  25.0 2.4 fusion.58
  34.0 2.5 %broadcast_in_dim.31 = bf16[16,32,2048]{2,1,0:T(8,128)(2,1)} broadcast(bf16[32,2048]{1,0:T(8,128)(2,1)} %get-tuple-element.25), dimensions={1,2} | broadcast | bytes 2228224 | tf_op jit(solution)/shard_map/broadcast_in_dim | solution.py:41
  36.5 5.4 %all-to-all-start.1 = ((bf16[16,32,2048]{2,1,0:T(8,128)(2,1)}), bf16[16,32,2048]{2,1,0:T(8,128)(2,1)}, u32[]{:S(2)}, u32[]{:S(2)}) async-start(bf16[16,32,2048]{2,1,0:T(8,128)(2,1)} %broadcast_in_dim.31), calls=%async_computation.1 | async-start | bytes 4194304 | tf_op jit(solution)/shard_map/all_to_all | solution.py:42
  45.5 12.2 %collective-permute-start.3 = (f32[128,128]{1,0:T(8,128)S(1)}, f32[128,128]{1,0:T(8,128)S(1)}, u32[]{:S(2)}, u32[]{:S(2)}) collective-permute-start(f32[128,128]{1,0:T(8,128)S(1)} %fusion.38), channel_id=1, source_target_pairs={{16,32},{48,64},{80,96},{112,128},{144,160},{176,192},{208,224},{2... | collective-permute-start | bytes 196616 | tf_op jit(solution)/shard_map/ppermute | solution.py:98
  57.7 2.6 %fusion = f32[2048,128]{0,1:T(8,128)S(1)} fusion(f32[2048,128]{0,1:T(8,128)} %copy.21, f32[128,2048]{1,0:T(8,128)} %param.7, f32[128,128]{1,0:T(8,128)} %fusion.36, f32[128,128]{1,0:T(8,128)S(1)} %fusion.38, pred[]{:T(512)S(6)} %eq.3), kind=kOutput, calls=%fused_computation.3 | convolution fusion | flops 402931712 | bytes 3276801 | tf_op jit(solution)/shard_map/dot_general | solution.py:20
  63.5 1.9 convolution_bitcast_fusion.4
  65.4 3.1 %convolution_bitcast_fusion.3 = f32[512,384]{0,1:T(8,128)S(1)} fusion(bf16[512,2048]{1,0:T(8,128)(2,1)} %bitcast.9, bf16[2048,128]{0,1:T(8,128)(2,1)} %copy-done.19, bf16[2048,128]{0,1:T(8,128)(2,1)} %copy-done.18, bf16[2048,128]{0,1:T(8,128)(2,1)} %copy-done.17), kind=kOutput, calls=%fused_computation.9 | convolution fusion | flops 810024960 | bytes 4456448 | tf_op jit(solution)/shard_map/dot_general | solution.py:113
  68.6 13.2 %collective-permute-start.5 = (f32[256,128]{0,1:T(8,128)S(1)}, f32[256,128]{0,1:T(8,128)S(1)}, u32[]{:S(2)}, u32[]{:S(2)}) collective-permute-start(f32[256,128]{0,1:T(8,128)S(1)} %slice_select_fusion.4), channel_id=1, source_target_pairs={{0,16},{16,0},{1,17},{17,1},{2,18},{18,2},{3,19},{19,3},{4,20},{20... | collective-permute-start | bytes 393224 | tf_op jit(solution)/shard_map/ppermute | solution.py:46
  83.4 1.9 collective-permute-start.4
  92.3 34.0 %all_to_all.30 = f32[8,72,128]{2,1,0:T(8,128)} all-to-all(f32[8,72,128]{2,1,0:T(8,128)S(1)} %pad_maximum_fusion.4), channel_id=1, replica_groups=mesh['far'=4,'near'=8,'core'=2,'vec'=16] {'near'}, dimensions={0} | all-to-all | bytes 589824 | tf_op jit(solution)/shard_map/all_to_all | solution.py:69
  127.3 44.0 %all_to_all.31 = f32[4,72,128]{2,1,0:T(8,128)S(1)} all-to-all(f32[4,72,128]{2,1,0:T(8,128)S(1)} %broadcast_in_dim.32), channel_id=1, replica_groups=mesh['far'=4,'near'=8,'core'=2,'vec'=16] {'far'}, dimensions={0} | all-to-all | bytes 294912 | tf_op jit(solution)/shard_map/all_to_all | solution.py:42
  172.7 23.1 %all_to_all.32 = f32[8,72,128]{2,1,0:T(8,128)S(1)} all-to-all(f32[8,72,128]{2,1,0:T(8,128)S(1)} %broadcast_in_dim.33), channel_id=1, replica_groups=mesh['far'=4,'near'=8,'core'=2,'vec'=16] {'near'}, dimensions={0} | all-to-all | bytes 589824 | tf_op jit(solution)/shard_map/all_to_all | solution.py:42
  195.8 8.8 %collective-permute-start.6 = (f32[8,72,128]{2,1,0:T(8,128)S(1)}, f32[8,72,128]{2,1,0:T(8,128)S(1)}, u32[]{:S(2)}, u32[]{:S(2)}) collective-permute-start(f32[8,72,128]{2,1,0:T(8,128)S(1)} %all_to_all.32), channel_id=1, source_target_pairs={{0,16},{16,0},{1,17},{17,1},{2,18},{18,2},{3,19},{19,3},{4,20},{20... | collective-permute-start | bytes 884744 | tf_op jit(solution)/shard_map/ppermute | solution.py:46
  207.7 4.5 %all-to-all-start.5 = ((f32[16,32,512]{2,1,0:T(8,128)}), f32[16,32,512]{2,1,0:T(8,128)}, u32[]{:S(2)}, u32[]{:S(2)}) async-start(f32[16,32,512]{2,1,0:T(8,128)} %broadcast_in_dim.34), calls=%async_computation.5 | async-start | bytes 2097152 | tf_op jit(solution)/shard_map/all_to_all | solution.py:42
  212.3 1.9 broadcast_select_fusion
  214.3 2.0 slice_select_fusion.3
  216.3 2.0 reduce-precision_convert_fusion.5
  218.3 2.7 %convolution_bitcast_fusion.1 = f32[2048,384]{0,1:T(8,128)} fusion(bf16[512,2048]{1,0:T(8,128)(2,1)S(1)} %bitcast.64, bf16[512,128]{0,1:T(8,128)(2,1)S(1)} %get-tuple-element.13, bf16[512,128]{0,1:T(8,128)(2,1)S(1)} %get-tuple-element.14, bf16[512,128]{0,1:T(8,128)(2,1)S(1)} %get-tuple-element.12), kind=kOutput, calls=%fused_computation.1 | convolution fusion | flops 806486016 | bytes 5636096 | tf_op jit(solution)/shard_map/dot_general | solution.py:125
  221.0 8.0 %all-to-all-done.5 = f32[16,32,512]{2,1,0:T(8,128)} async-done(((f32[16,32,512]{2,1,0:T(8,128)}), f32[16,32,512]{2,1,0:T(8,128)}, u32[]{:S(2)}, u32[]{:S(2)}) %all-to-all-start.5) | async-done | bytes 1048608 | tf_op jit(solution)/shard_map/all_to_all | solution.py:42
  229.0 2.3 fusion.59
  231.3 2.5 %reduce-precision_convert_fusion.3 = (bf16[512,128]{0,1:T(8,128)(2,1)S(1)}, bf16[512,128]{0,1:T(8,128)(2,1)S(1)}, bf16[512,128]{0,1:T(8,128)(2,1)S(1)}) fusion(f32[512,128]{1,0:T(8,128)S(1)} %fusion.59, f32[256,128]{1,0:T(8,128)} %bitcast.72, f32[256,128]{1,0:T(8,128)S(1)} %bitcast.71, f32[2,512,512]{2,1,0:T(8,128)} %copy-done.2), kind=kOutput, calls=%fused_computation.43 | convolution fusion | flops 403243008 | bytes 1966080 | tf_op jit(solution)/shard_map/dot_general | solution.py:16
  233.7 2.7 %convolution_bitcast_fusion = f32[2048,384]{0,1:T(8,128)S(1)} fusion(bf16[512,2048]{1,0:T(8,128)(2,1)} %bitcast.9, bf16[512,128]{0,1:T(8,128)(2,1)S(1)} %get-tuple-element.16, bf16[512,128]{0,1:T(8,128)(2,1)S(1)} %get-tuple-element.17, bf16[512,128]{0,1:T(8,128)(2,1)S(1)} %get-tuple-element.15), kind=kOutput, calls=%fused_computation | convolution fusion | flops 806486016 | bytes 5636096 | tf_op jit(solution)/shard_map/dot_general | solution.py:125
  (94 shorter events, 34.3 us)
Async XLA Ops:
  0.0 11.0 %copy-start = (f32[128,512]{1,0:T(8,128)S(1)}, f32[128,512]{1,0:T(8,128)}, u32[]{:S(2)}) copy-start(f32[128,512]{1,0:T(8,128)} %param.8) | copy-start | bytes 786436
  3.3 7.7 %copy-start.3 = (f32[2048,128]{1,0:T(8,128)S(1)}, f32[2048,128]{1,0:T(8,128)}, u32[]{:S(2)}) copy-start(f32[2048,128]{1,0:T(8,128)} %param.6) | copy-start | bytes 3145732
  3.3 30.7 %all-to-all-start = ((bf16[16,32,2048]{2,1,0:T(8,128)(2,1)}), bf16[16,32,2048]{2,1,0:T(8,128)(2,1)S(1)}, u32[]{:S(2)}, u32[]{:S(2)}) async-start(bf16[16,32,2048]{2,1,0:T(8,128)(2,1)} %broadcast_in_dim.30), calls=%async_computation | async-start | bytes 4194304 | tf_op jit(solution)/shard_map/all_to_all | solution.py:42
  11.0 16.3 %copy-start.21 = (f32[1,128,128]{2,1,0:T(8,128)S(1)}, f32[1,128,128]{2,1,0:T(8,128)}, u32[]{:S(2)}) copy-start(f32[1,128,128]{2,1,0:T(8,128)} %param.9) | copy-start | bytes 196612
  11.4 15.9 %collective-permute-start = (f32[128,128]{1,0:T(8,128)S(1)}, f32[128,128]{1,0:T(8,128)S(1)}, u32[]{:S(2)}, u32[]{:S(2)}) collective-permute-start(f32[128,128]{1,0:T(8,128)S(1)} %fusion.31), channel_id=1, source_target_pairs={{16,0},{48,32},{80,64},{112,96},{144,128},{176,160},{208,192},{240... | collective-permute-start | bytes 196616 | tf_op jit(solution)/shard_map/ppermute | solution.py:92
  29.9 13.4 %collective-permute-start.2 = (f32[128,128]{1,0:T(8,128)}, f32[128,128]{1,0:T(8,128)}, u32[]{:S(2)}, u32[]{:S(2)}) collective-permute-start(f32[128,128]{1,0:T(8,128)} %convolution_subtract_fusion), channel_id=1, source_target_pairs={{0,1008},{32,16},{64,48},{96,80},{128,112},{160,144},{192,176},{22... | collective-permute-start | bytes 196616 | tf_op jit(solution)/shard_map/ppermute | solution.py:96
  31.2 12.1 %collective-permute-start.1 = (f32[128,128]{1,0:T(8,128)}, f32[128,128]{1,0:T(8,128)}, u32[]{:S(2)}, u32[]{:S(2)}) collective-permute-start(f32[128,128]{1,0:T(8,128)} %fusion.36), channel_id=1, source_target_pairs={{0,16},{32,48},{64,80},{96,112},{128,144},{160,176},{192,208},{224... | collective-permute-start | bytes 196616 | tf_op jit(solution)/shard_map/ppermute | solution.py:94
  36.5 28.8 %all-to-all-start.1 = ((bf16[16,32,2048]{2,1,0:T(8,128)(2,1)}), bf16[16,32,2048]{2,1,0:T(8,128)(2,1)}, u32[]{:S(2)}, u32[]{:S(2)}) async-start(bf16[16,32,2048]{2,1,0:T(8,128)(2,1)} %broadcast_in_dim.31), calls=%async_computation.1 | async-start | bytes 4194304 | tf_op jit(solution)/shard_map/all_to_all | solution.py:42
  45.5 14.9 %collective-permute-start.3 = (f32[128,128]{1,0:T(8,128)S(1)}, f32[128,128]{1,0:T(8,128)S(1)}, u32[]{:S(2)}, u32[]{:S(2)}) collective-permute-start(f32[128,128]{1,0:T(8,128)S(1)} %fusion.38), channel_id=1, source_target_pairs={{16,32},{48,64},{80,96},{112,128},{144,160},{176,192},{208,224},{2... | collective-permute-start | bytes 196616 | tf_op jit(solution)/shard_map/ppermute | solution.py:98
  60.4 1.6 copy-start.12
  65.4 16.5 %copy-start.7 = (f32[512,384]{0,1:T(8,128)S(1)}, f32[512,384]{0,1:T(8,128)}, u32[]{:S(2)}) copy-start(f32[512,384]{0,1:T(8,128)} %convolution_bitcast_fusion.4) | copy-start | bytes 2359300
  68.5 13.5 %copy-start.6 = (f32[32,512]{0,1:T(8,128)S(1)}, f32[32,512]{0,1:T(8,128)}, u32[]{:S(2)}) copy-start(f32[32,512]{0,1:T(8,128)} %fusion.53) | copy-start | bytes 196612
  68.6 16.7 %collective-permute-start.5 = (f32[256,128]{0,1:T(8,128)S(1)}, f32[256,128]{0,1:T(8,128)S(1)}, u32[]{:S(2)}, u32[]{:S(2)}) collective-permute-start(f32[256,128]{0,1:T(8,128)S(1)} %slice_select_fusion.4), channel_id=1, source_target_pairs={{0,16},{16,0},{1,17},{17,1},{2,18},{18,2},{3,19},{19,3},{4,20},{20... | collective-permute-start | bytes 393224 | tf_op jit(solution)/shard_map/ppermute | solution.py:46
  82.0 3.3 %copy-start.14 = (f32[32,128]{0,1:T(8,128)}, f32[32,128]{0,1:T(8,128)S(1)}, u32[]{:S(2)}) copy-start(f32[32,128]{0,1:T(8,128)S(1)} %get-tuple-element.21) | copy-start | bytes 49156
  82.1 3.3 %copy-start.15 = (f32[32,128]{0,1:T(8,128)}, f32[32,128]{0,1:T(8,128)S(1)}, u32[]{:S(2)}) copy-start(f32[32,128]{0,1:T(8,128)S(1)} %get-tuple-element.22) | copy-start | bytes 49156
  82.1 3.3 %copy-start.16 = (f32[32,128]{0,1:T(8,128)}, f32[32,128]{0,1:T(8,128)S(1)}, u32[]{:S(2)}) copy-start(f32[32,128]{0,1:T(8,128)S(1)} %get-tuple-element.23) | copy-start | bytes 49156
  83.4 4.3 %collective-permute-start.4 = (f32[320,128]{0,1:T(8,128)}, f32[320,128]{0,1:T(8,128)}, u32[]{:S(2)}, u32[]{:S(2)}) collective-permute-start(f32[320,128]{0,1:T(8,128)} %fusion.33), channel_id=1, source_target_pairs={{0,16},{16,0},{1,17},{17,1},{2,18},{18,2},{3,19},{19,3},{4,20},{20... | collective-permute-start | bytes 491528 | tf_op jit(solution)/shard_map/ppermute | solution.py:46
  195.8 10.0 %copy-start.5 = (f32[8,72,128]{2,1,0:T(8,128)}, f32[8,72,128]{2,1,0:T(8,128)S(1)}, u32[]{:S(2)}) copy-start(f32[8,72,128]{2,1,0:T(8,128)S(1)} %all_to_all.32) | copy-start | bytes 884740
  195.8 9.9 %collective-permute-start.6 = (f32[8,72,128]{2,1,0:T(8,128)S(1)}, f32[8,72,128]{2,1,0:T(8,128)S(1)}, u32[]{:S(2)}, u32[]{:S(2)}) collective-permute-start(f32[8,72,128]{2,1,0:T(8,128)S(1)} %all_to_all.32), channel_id=1, source_target_pairs={{0,16},{16,0},{1,17},{17,1},{2,18},{18,2},{3,19},{19,3},{4,20},{20... | collective-permute-start | bytes 884744 | tf_op jit(solution)/shard_map/ppermute | solution.py:46
  207.7 21.3 %all-to-all-start.5 = ((f32[16,32,512]{2,1,0:T(8,128)}), f32[16,32,512]{2,1,0:T(8,128)}, u32[]{:S(2)}, u32[]{:S(2)}) async-start(f32[16,32,512]{2,1,0:T(8,128)} %broadcast_in_dim.34), calls=%async_computation.5 | async-start | bytes 2097152 | tf_op jit(solution)/shard_map/all_to_all | solution.py:42
  212.3 2.0 copy-start.11
  212.3 2.0 copy-start.9
  214.3 2.0 copy-start.2
  233.7 2.7 %copy-start.1 = (f32[2048,384]{0,1:T(8,128)S(1)}, f32[2048,384]{0,1:T(8,128)}, u32[]{:S(2)}) copy-start(f32[2048,384]{0,1:T(8,128)} %convolution_bitcast_fusion.1) | copy-start | bytes 9437188
  (8 other events, 8.7 us)

commit v2 on v1

v2 whole, which is shorter than its diff:
```python
import functools

import jax
import jax.numpy as jnp
from jax import lax
from jax.experimental import pallas as pl
from jax.experimental.pallas import tpu as pltpu
from jax.sharding import Mesh
from jax.sharding import PartitionSpec as P

ROW = ("far", "near", "core")
HIGHEST = lax.Precision.HIGHEST
F32 = jnp.float32
BF16 = jnp.bfloat16


def product(left, right):
    return jnp.dot(left, right, precision=HIGHEST, preferred_element_type=F32)


def product_t(left, right):
    return lax.dot_general(left, right, (((0,), (0,)), ((), ())), precision=HIGHEST, preferred_element_type=F32)


def product_nt(left, right):
    return lax.dot_general(left, right, (((1,), (1,)), ((), ())), precision=HIGHEST, preferred_element_type=F32)


def store_thirds(target, array):
    width = array.shape[1]
    high = array.astype(BF16)
    rest = array - high.astype(F32)
    mid = rest.astype(BF16)
    target[:, :width] = high
    target[:, width : 2 * width] = mid
    target[:, 2 * width :] = (rest - mid.astype(F32)).astype(BF16)


def fold(wide):
    width = wide.shape[1] // 3
    return wide[:, :width] + (wide[:, width : 2 * width] + wide[:, 2 * width :])


def to_everyone(array, axis):
    copies = jnp.broadcast_to(array, (lax.axis_size(axis), *array.shape))
    return lax.all_to_all(copies, axis, split_axis=0, concat_axis=0, tiled=True)


def swapped(array):
    return lax.ppermute(array, "core", [(0, 1), (1, 0)])


def project_kernel(core_ref, panel_ref, own_ref, current_ref, send_ref, keep_ref, split):
    del core_ref
    step = pl.program_id(0)

    @pl.when(step == 0)
    def _():
        store_thirds(split, current_ref[...])

    rows = panel_ref.shape[0] * panel_ref.shape[1]
    own, width = own_ref.shape[0], current_ref.shape[1]
    tiles = rows // width
    gram_end = rows + own * tiles
    panel = panel_ref[...].reshape(rows, panel_ref.shape[2])
    part = fold(jnp.dot(panel, split[...], preferred_element_type=F32))
    for which, out_ref in enumerate((send_ref, keep_ref)):

        @pl.when(step == 2 * which)
        def _(out_ref=out_ref):
            out_ref[:rows] = part
            gram = lax.dot_general(own_ref[...], panel, (((1,), (1,)), ((), ())), preferred_element_type=F32)
            for t in range(tiles):
                out_ref[rows + own * t : rows + own * (t + 1)] = gram[:, width * t : width * (t + 1)]

        @pl.when(step == 2 * which + 1)
        def _(out_ref=out_ref):
            out_ref[gram_end:] = part


def project(core, panels, panel_vectors, current):
    sources, _, own, depth_rows = panels.shape
    rows, width = sources // 2 * own, current.shape[1]
    total = 2 * rows + own * (rows // width)
    whole = pl.BlockSpec((total, width), lambda i, c: (0, 0))
    flops = 2 * 2 * sources * own * depth_rows * width * 3
    return pl.pallas_call(
        project_kernel,
        out_shape=[jax.ShapeDtypeStruct((total, width), F32)] * 2,
        grid_spec=pltpu.PrefetchScalarGridSpec(
            num_scalar_prefetch=1,
            grid=(4,),
            in_specs=[
                pl.BlockSpec(
                    (sources // 2, None, own, depth_rows),
                    lambda i, c: (jnp.where(i < 2, 1 - c[0], c[0]), i % 2, 0, 0),
                ),
                pl.BlockSpec((None, own, depth_rows), lambda i, c: (1, 0, 0)),
                pl.BlockSpec(current.shape, lambda i, c: (0, 0)),
            ],
            out_specs=[whole, whole],
            scratch_shapes=[pltpu.VMEM((depth_rows, 3 * width), BF16)],
        ),
        cost_estimate=pl.CostEstimate(flops=flops, bytes_accessed=panels.size * 2 + current.size * 4, transcendentals=0),
        name="project",
    )(core, panels, panel_vectors, current)


def apply_kernel(first_row, corrections, core_ref, mine_ref, other_ref, factor_ref, panel_ref, current_ref, *refs):
    correction_refs, (weights_ref, out_ref, total, split) = refs[:corrections], refs[corrections:]
    depth = factor_ref.shape[0]
    half = depth // 2

    @pl.when(pl.program_id(0) == 0)
    def _():
        for which, (low_ref, high_ref) in enumerate(((mine_ref, other_ref), (other_ref, mine_ref))):

            @pl.when(core_ref[0] == which)
            def _(low_ref=low_ref, high_ref=high_ref):
                total[:half] = low_ref[first_row : first_row + half]
                total[half:] = high_ref[first_row : first_row + half]

        wanted = total[...]
        if corrections:
            wanted = wanted - (correction_refs[0][...] + correction_refs[1][...])
        row = lax.broadcasted_iota(jnp.int32, (depth, depth), 0)
        column = lax.broadcasted_iota(jnp.int32, (depth, depth), 1)
        factor = jnp.where(row <= column, factor_ref[...], 0.0)
        weights = product(factor, wanted)
        weights_ref[...] = weights
        store_thirds(split, weights)

    panel = panel_ref[...].reshape(depth, panel_ref.shape[2])
    update = lax.dot_general(panel, split[...], (((0,), (0,)), ((), ())), preferred_element_type=F32)
    out_ref[...] = current_ref[...] - fold(update)


def apply_panel(core, mine, other, panel_factor, panels, current, index, first_row, corrections=()):
    sources, _, own, n_rows = panels.shape
    depth, width = panel_factor.shape[1], current.shape[1]
    steps = 4
    block = n_rows // steps
    whole = lambda array: pl.BlockSpec(array.shape, lambda i, c: (0, 0))
    flops = 2 * n_rows * depth * width * 3 + 2 * depth * depth * width * 6
    return pl.pallas_call(
        functools.partial(apply_kernel, first_row, len(corrections)),
        out_shape=[jax.ShapeDtypeStruct((depth, width), F32), jax.ShapeDtypeStruct(current.shape, F32)],
        grid_spec=pltpu.PrefetchScalarGridSpec(
            num_scalar_prefetch=1,
            grid=(steps,),
            in_specs=[
                whole(mine),
                whole(other),
                pl.BlockSpec((None, depth, depth), lambda i, c: (index, 0, 0)),
                pl.BlockSpec((sources, None, own, block), lambda i, c: (0, index, 0, i)),
                pl.BlockSpec((block, width), lambda i, c: (i, 0)),
                *[whole(array) for array in corrections],
            ],
            out_specs=[
                pl.BlockSpec((depth, width), lambda i, c: (0, 0)),
                pl.BlockSpec((block, width), lambda i, c: (i, 0)),
            ],
            scratch_shapes=[pltpu.VMEM((depth, width), F32), pltpu.VMEM((depth, 3 * width), BF16)],
        ),
        cost_estimate=pl.CostEstimate(flops=flops, bytes_accessed=panels.size + current.size * 8, transcendentals=0),
        name="apply_panel",
    )(core, mine, other, panel_factor, panels, current, *corrections)


def couple_kernel(core_ref, gram_ref, weights_ref, out_ref):
    sources, rows, width = gram_ref.shape
    depth = weights_ref.shape[0]
    tiles = depth // 2 // width
    own = rows // tiles
    result = None
    for t in range(tiles):
        gram = gram_ref[:, own * t : own * (t + 1)].reshape(sources * own, width)
        start = pl.multiple_of(core_ref[0] * (depth // 2) + width * t, width)
        term = product(gram, weights_ref[pl.ds(start, width)])
        result = term if result is None else result + term
    out_ref[...] = result


def couple(core, gram, weights):
    return pl.pallas_call(
        couple_kernel,
        out_shape=jax.ShapeDtypeStruct(weights.shape, F32),
        in_specs=[pl.BlockSpec(memory_space=pltpu.SMEM)] + [pl.BlockSpec(memory_space=pltpu.VMEM)] * 2,
        out_specs=pl.BlockSpec(memory_space=pltpu.VMEM),
        cost_estimate=pl.CostEstimate(flops=weights.size * weights.shape[0] * 6, bytes_accessed=gram.size * 4, transcendentals=0),
        name="couple",
    )(core, gram, weights)


def on_device(vectors, band_head, band_tail, band_factor, panel_vectors, panel_factor):
    margin = band_tail.shape[1]
    width = vectors.shape[1]
    depth = panel_factor.shape[1]
    core_index = lax.axis_index("core")
    even = core_index == 0
    core = core_index.astype(jnp.int32).reshape(1)
    n = lax.axis_size(ROW)

    panels = to_everyone(panel_vectors, "vec")

    factor = jnp.triu(band_factor[0])
    own = product(band_head, vectors)
    tail = product(band_tail, vectors[:margin])
    cross = product_nt(band_tail, band_head[:, :margin])
    tail_next = lax.ppermute(tail, ROW, [(i + 1, i) for i in range(0, n, 2)])
    weights_a = product(factor, own + tail_next)
    weights_a_prev = lax.ppermute(weights_a, ROW, [(i, i + 1) for i in range(0, n, 2)])
    tail_b = tail - product(cross, weights_a)
    tail_b_next = lax.ppermute(tail_b, ROW, [(i, (i - 1) % n) for i in range(0, n, 2)])
    weights_b = product(factor, own - product_t(cross, weights_a_prev) + tail_b_next)
    weights_b_prev = lax.ppermute(weights_b, ROW, [(i, (i + 1) % n) for i in range(1, n, 2)])
    weights_own = jnp.where(even, weights_a, weights_b)
    weights_prev = jnp.where(even, weights_b_prev, weights_a_prev)
    current = vectors - product_t(band_head, weights_own)
    top = current[:margin] - product_t(band_tail, weights_prev)
    current = jnp.concatenate([top, current[margin:]], axis=0)

    send, keep = project(core, panels, panel_vectors, current)
    group = lax.axis_size("near")
    blocks = (keep + swapped(send)).reshape(group, -1, width)
    share = jnp.sum(lax.all_to_all(blocks, "near", split_axis=0, concat_axis=0, tiled=True), axis=0)
    share = jnp.sum(to_everyone(share, "far"), axis=0)
    mine = to_everyone(share, "near").reshape(-1, width)
    half = depth // 2
    gram_end = mine.shape[0] - half
    gram = to_everyone(mine[half:gram_end], "vec")
    other = swapped(mine)

    weights0, current = apply_panel(core, mine, other, panel_factor, panels, current, 0, 0)
    coupled = couple(core, gram, weights0)
    corrections = (coupled, swapped(coupled))
    _, result = apply_panel(core, mine, other, panel_factor, panels, current, 1, gram_end, corrections)
    return result


def solution(mesh):
    devices = mesh.devices.reshape(4, 8, 2, mesh.shape["vec"])
    split = Mesh(devices, ("far", "near", "core", "vec"))
    return jax.shard_map(
        on_device,
        mesh=split,
        in_specs=(
            P(ROW, "vec"),
            P(None, ROW),
            P(None, ROW),
            P(ROW, None, None),
            P(None, "vec", ROW),
            P(),
        ),
        out_specs=P(ROW, "vec"),
        check_vma=False,
    )
```

time: 240 us -> 221 us (0.921)
  matrix products: 31.3 us -> 5.3 us
  Pallas kernels: 0 us -> 21.9 us
  waiting for transfers between devices: 9.87 us -> 27 us
  starting transfers between devices: 68.5 us -> 53.8 us
  other arithmetic: 11.9 us -> 2.08 us
  local copies, waits for them, and re-layouts: 15.3 us -> 6.76 us
    pallas_call x0 -> x4, Pallas kernels: none -> 21.9 us  [the longest x2 12.5 us: apply_panel(): pl.pallas_call(functools.partial(apply_kernel, first_row, len(corrections...]
    dot_general x5 -> x0, matrix products: 11.8 us -> none  [the longest x2 5.38 us: spread(): lax.dot_general(panel, thirds(w), (((0,), (0,)), ((), ())), preferred_ele...]
    ppermute x1, starting transfers between devices: 12.2 us -> 1.29 us  [on_device(): lax.ppermute(weights_b, ROW, [(i, (i + 1) % n) for i in range(1, n, 2)])]
    dot_general x8 -> x5, matrix products: 13.1 us -> 2.24 us  [product(): return jnp.dot(left, right, precision=HIGHEST, preferred_element_type=F32)]
    all_to_all x3 -> x2, starting transfers between devices: 17.6 us -> 12.1 us  [to_everyone(): return lax.all_to_all(copies, axis, split_axis=0, concat_axis=0, tiled=True)]
    all_to_all x3 -> x2, waiting for transfers between devices: 9.59 us -> 15 us  [to_everyone(): return lax.all_to_all(copies, axis, split_axis=0, concat_axis=0, tiled=True)]
    ppermute x1, waiting for transfers between devices: 0.01 us -> 4.77 us  [on_device(): lax.ppermute(weights_a, ROW, [(i, i + 1) for i in range(0, n, 2)])]
    select_n x5 -> x0, other arithmetic: 4.76 us -> none  [the longest x2 2.01 us: joined(): jnp.where(first, mine, other)]
  transfers between devices with their start and end apart: 10 -> 9, of which waited for: 3 -> 6; matrix products, arithmetic and copies ran while one was open for 14% -> 3% of each run, Pallas kernels for 0% -> 3%
where the time goes in v2:
time: 221 us; the launch traced here: 220 us
  blocking collectives  103 us (47%)
  starting transfers between devices  53.8 us (24%)
  waiting for transfers between devices  27 us (12%)
  Pallas kernels  21.9 us (10%)
  local copies, waits for them, and re-layouts  6.76 us (3%)
  matrix products  5.3 us (2%)
    all_to_all x2, blocking collectives, to_everyone(): return lax.all_to_all(copies, axis, split_axis=0, concat_axis=0, tiled=True)  66.7 us
    all_to_all x1, blocking collectives, on_device(): lax.all_to_all(blocks, 'near', split_axis=0, concat_axis=0, tiled=True)  36.3 us
    ppermute x3, starting transfers between devices, swapped(): return lax.ppermute(array, 'core', [(0, 1), (1, 0)])  24.9 us
    all_to_all x2, waiting for transfers between devices, to_everyone(): return lax.all_to_all(copies, axis, split_axis=0, concat_axis=0, tiled=True)  15 us
    ppermute x1, starting transfers between devices, on_device(): tail_next = lax.ppermute(tail, ROW, [(i + 1, i) for i in range(0, n, 2)])  12.9 us
    pallas_call x2, Pallas kernels, apply_panel(): pl.pallas_call(functools.partial(apply_kernel, first_row, len(corrections...  12.5 us
    all_to_all x2, starting transfers between devices, to_everyone(): return lax.all_to_all(copies, axis, split_axis=0, concat_axis=0, tiled=True)  12.1 us
    pallas_call x1, Pallas kernels, project(): pl.pallas_call(project_kernel, out_shape=[jax.ShapeDtypeStruct((total, wi...  6.93 us
  transfers between devices with their start and end apart: 9, of which 6 were waited for; matrix products, arithmetic and copies ran while one was open for 3% of the time, Pallas kernels for 3%

profile of v2, /device:TPU:1, one launch (start us, length us, event | category | flops | bytes accessed | tf_op | source)
XLA Modules:
  0.0 220.1 jit_solution(6785369762473737571)
XLA Ops:
  0.0 3.5 %broadcast_in_dim.16 = bf16[16,2,32,2048]{3,2,1,0:T(8,128)(2,1)} broadcast(bf16[2,32,2048]{2,1,0:T(8,128)(2,1)} %own_ref.1), dimensions={1,2,3} | broadcast | bytes 4456448 | tf_op jit(solution)/shard_map/broadcast_in_dim | solution.py:45
  3.5 7.8 %all-to-all-start = ((bf16[16,2,32,2048]{3,2,1,0:T(8,128)(2,1)}), bf16[16,2,32,2048]{3,2,1,0:T(8,128)(2,1)}, u32[]{:S(2)}, u32[]{:S(2)}) async-start(bf16[16,2,32,2048]{3,2,1,0:T(8,128)(2,1)} %broadcast_in_dim.16), calls=%async_computation | async-start | bytes 8388608 | tf_op jit(solution)/shard_map/all_to_all | solution.py:46
  11.7 12.9 %collective-permute-start = (f32[128,128]{1,0:T(8,128)S(1)}, f32[128,128]{1,0:T(8,128)S(1)}, u32[]{:S(2)}, u32[]{:S(2)}) collective-permute-start(f32[128,128]{1,0:T(8,128)S(1)} %fusion.5), channel_id=1, source_target_pairs={{16,0},{48,32},{80,64},{112,96},{144,128},{176,160},{208,192},{240... | collective-permute-start | bytes 196616 | tf_op jit(solution)/shard_map/ppermute | solution.py:210
  26.7 1.3 collective-permute-start.2
  28.0 1.3 collective-permute-start.1
  29.3 3.4 %collective-permute-done.2 = f32[128,128]{1,0:T(8,128)S(1)} collective-permute-done((f32[128,128]{1,0:T(8,128)S(1)}, f32[128,128]{1,0:T(8,128)S(1)}, u32[]{:S(2)}, u32[]{:S(2)}) %collective-permute-start.2) | collective-permute-done | bytes 65568 | tf_op jit(solution)/shard_map/ppermute | solution.py:214
  32.7 4.8 %collective-permute-done.1 = f32[128,128]{1,0:T(8,128)S(1)} collective-permute-done((f32[128,128]{1,0:T(8,128)S(1)}, f32[128,128]{1,0:T(8,128)S(1)}, u32[]{:S(2)}, u32[]{:S(2)}) %collective-permute-start.1) | collective-permute-done | bytes 65568 | tf_op jit(solution)/shard_map/ppermute | solution.py:212
  38.0 1.3 collective-permute-start.3
  39.3 1.8 fusion
  42.8 15.0 %all-to-all-done.panel_ref = bf16[16,2,32,2048]{3,2,1,0:T(8,128)(2,1)} async-done(((bf16[16,2,32,2048]{3,2,1,0:T(8,128)(2,1)}), bf16[16,2,32,2048]{3,2,1,0:T(8,128)(2,1)}, u32[]{:S(2)}, u32[]{:S(2)}) %all-to-all-start) | async-done | bytes 4194336 | tf_op jit(solution)/shard_map/all_to_all | solution.py:46
  57.8 6.9 %project.1 = (f32[576,128]{1,0:T(8,128)}, f32[576,128]{1,0:T(8,128)}) custom-call(s32[1]{0:T(128)} %bitcast.core_ref, bf16[16,2,32,2048]{3,2,1,0:T(8,128)(2,1)} %all-to-all-done.panel_ref, bf16[2,32,2048]{2,1,0:T(8,128)(2,1)} %own_ref.1, f32[2048,128]{1,0:T(8,128)} %pad_maximum_fusion.current_ref), custom_call_target="tpu_custom_call" | custom-call | flops 1610612736 | bytes 5242880 | tf_op jit(solution)/shard_map/project/pallas_call | solution.py:87
  64.7 13.5 %collective-permute-start.4 = (f32[576,128]{1,0:T(8,128)}, f32[576,128]{1,0:T(8,128)S(1)}, u32[]{:S(2)}, u32[]{:S(2)}) collective-permute-start(f32[576,128]{1,0:T(8,128)} %get-tuple-element.11), channel_id=1, source_target_pairs={{0,16},{16,0},{1,17},{17,1},{2,18},{18,2},{3,19},{19,3},{4,20},{20... | collective-permute-start | bytes 884744 | tf_op jit(solution)/shard_map/ppermute | solution.py:50
  78.2 1.4 collective-permute-done.4
  80.6 36.3 %all_to_all.25 = f32[8,72,128]{2,1,0:T(8,128)S(1)} all-to-all(f32[8,72,128]{2,1,0:T(8,128)S(1)} %bitcast.30), channel_id=1, replica_groups=mesh['far'=4,'near'=8,'core'=2,'vec'=16] {'near'}, dimensions={0} | all-to-all | bytes 589824 | tf_op jit(solution)/shard_map/all_to_all | solution.py:226
  117.0 42.2 %all_to_all.26 = f32[4,72,128]{2,1,0:T(8,128)S(1)} all-to-all(f32[4,72,128]{2,1,0:T(8,128)S(1)} %broadcast_in_dim.18), channel_id=1, replica_groups=mesh['far'=4,'near'=8,'core'=2,'vec'=16] {'far'}, dimensions={0} | all-to-all | bytes 294912 | tf_op jit(solution)/shard_map/all_to_all | solution.py:46
  159.2 24.5 %all_to_all.27 = f32[8,72,128]{2,1,0:T(8,128)S(1)} all-to-all(f32[8,72,128]{2,1,0:T(8,128)S(1)} %broadcast_in_dim.19), channel_id=1, replica_groups=mesh['far'=4,'near'=8,'core'=2,'vec'=16] {'near'}, dimensions={0} | all-to-all | bytes 589824 | tf_op jit(solution)/shard_map/all_to_all | solution.py:46
  184.6 4.4 %all-to-all-start.4 = ((f32[16,64,128]{2,1,0:T(8,128)}), f32[16,64,128]{2,1,0:T(8,128)S(1)}, u32[]{:S(2)}, u32[]{:S(2)}) async-start(f32[16,64,128]{2,1,0:T(8,128)} %broadcast_in_dim.20), calls=%async_computation.4 | async-start | bytes 1048576 | tf_op jit(solution)/shard_map/all_to_all | solution.py:46
  189.0 9.0 %collective-permute-start.5 = (f32[576,128]{1,0:T(8,128)S(1)}, f32[576,128]{1,0:T(8,128)S(1)}, u32[]{:S(2)}, u32[]{:S(2)}) collective-permute-start(f32[576,128]{1,0:T(8,128)S(1)} %bitcast.27), channel_id=1, source_target_pairs={{0,16},{16,0},{1,17},{17,1},{2,18},{18,2},{3,19},{19,3},{4,20},{20... | collective-permute-start | bytes 884744 | tf_op jit(solution)/shard_map/ppermute | solution.py:50
  198.1 1.2 collective-permute-done.5.other_ref
  200.0 6.2 %apply_panel.2 = (f32[512,128]{1,0:T(8,128)}, f32[2048,128]{1,0:T(8,128)}) custom-call(s32[1]{0:T(128)} %bitcast.core_ref, f32[576,128]{1,0:T(8,128)} %bitcast.28, f32[576,128]{1,0:T(8,128)} %copy-done.5, f32[2,512,512]{2,1,0:T(8,128)} %factor_ref.3, bf16[16,2,32,2048]{3,2,1,0:T(8,128)(2,1)} %all-to-all-done.panel_ref, f32[2048,128]{1,0:T(8,128)} %pad_maximum_fusion.current_ref), custom_call_target="tpu_custom_call" | custom-call | flops 1207959552 | bytes 4194304 | tf_op jit(solution)/shard_map/apply_panel/pallas_call | solution.py:145
  206.9 2.4 %couple.1.refs_0_ = f32[512,128]{1,0:T(8,128)} custom-call(s32[1]{0:T(128)} %bitcast.core_ref, f32[16,64,128]{2,1,0:T(8,128)} %copy-done.4, f32[512,128]{1,0:T(8,128)} %get-tuple-element.13.weights_ref), custom_call_target="tpu_custom_call" | custom-call | flops 201326592 | bytes 524288 | tf_op jit(solution)/shard_map/couple/pallas_call | solution.py:185
  209.4 2.3 %collective-permute-start.6 = (f32[512,128]{1,0:T(8,128)}, f32[512,128]{1,0:T(8,128)S(1)}, u32[]{:S(2)}, u32[]{:S(2)}) collective-permute-start(f32[512,128]{1,0:T(8,128)} %couple.1.refs_0_), channel_id=1, source_target_pairs={{0,16},{16,0},{1,17},{17,1},{2,18},{18,2},{3,19},{19,3},{4,20},{20... | collective-permute-start | bytes 786440 | tf_op jit(solution)/shard_map/ppermute | solution.py:50
  211.6 1.4 collective-permute-done.6.refs_1_
  213.7 6.3 %apply_panel.3 = (f32[512,128]{1,0:T(8,128)}, f32[2048,128]{1,0:T(8,128)}) custom-call(s32[1]{0:T(128)} %bitcast.core_ref, f32[576,128]{1,0:T(8,128)} %bitcast.29, f32[576,128]{1,0:T(8,128)} %copy-done.5, f32[2,512,512]{2,1,0:T(8,128)} %factor_ref.3, bf16[16,2,32,2048]{3,2,1,0:T(8,128)(2,1)} %all-to-all-done.panel_ref, ...), custom_call_target="tpu_custom_call" | custom-call | flops 1207959552 | bytes 4194304 | tf_op jit(solution)/shard_map/apply_panel/pallas_call | solution.py:145
  (37 shorter events, 8.8 us)
Async XLA Ops:
  0.0 11.3 %copy-start = (f32[128,512]{1,0:T(8,128)S(1)}, f32[128,512]{1,0:T(8,128)}, u32[]{:S(2)}) copy-start(f32[128,512]{1,0:T(8,128)} %param.8) | copy-start | bytes 786436
  3.5 7.8 %copy-start.1 = (f32[2048,128]{1,0:T(8,128)S(1)}, f32[2048,128]{1,0:T(8,128)}, u32[]{:S(2)}) copy-start(f32[2048,128]{1,0:T(8,128)} %param.6) | copy-start | bytes 3145732
  3.5 21.1 %copy-start.2 = (f32[128,2048]{1,0:T(8,128)S(1)}, f32[128,2048]{1,0:T(8,128)}, u32[]{:S(2)}) copy-start(f32[128,2048]{1,0:T(8,128)} %param.7) | copy-start | bytes 3145732
  3.5 22.7 %copy-start.7 = (f32[1,128,128]{2,1,0:T(8,128)S(1)}, f32[1,128,128]{2,1,0:T(8,128)}, u32[]{:S(2)}) copy-start(f32[1,128,128]{2,1,0:T(8,128)} %param.9) | copy-start | bytes 196612
  3.5 54.2 %all-to-all-start = ((bf16[16,2,32,2048]{3,2,1,0:T(8,128)(2,1)}), bf16[16,2,32,2048]{3,2,1,0:T(8,128)(2,1)}, u32[]{:S(2)}, u32[]{:S(2)}) async-start(bf16[16,2,32,2048]{3,2,1,0:T(8,128)(2,1)} %broadcast_in_dim.16), calls=%async_computation | async-start | bytes 8388608 | tf_op jit(solution)/shard_map/all_to_all | solution.py:46
  11.7 14.5 %collective-permute-start = (f32[128,128]{1,0:T(8,128)S(1)}, f32[128,128]{1,0:T(8,128)S(1)}, u32[]{:S(2)}, u32[]{:S(2)}) collective-permute-start(f32[128,128]{1,0:T(8,128)S(1)} %fusion.5), channel_id=1, source_target_pairs={{16,0},{48,32},{80,64},{112,96},{144,128},{176,160},{208,192},{240... | collective-permute-start | bytes 196616 | tf_op jit(solution)/shard_map/ppermute | solution.py:210
  26.7 6.0 %collective-permute-start.2 = (f32[128,128]{1,0:T(8,128)S(1)}, f32[128,128]{1,0:T(8,128)S(1)}, u32[]{:S(2)}, u32[]{:S(2)}) collective-permute-start(f32[128,128]{1,0:T(8,128)S(1)} %convolution_subtract_fusion), channel_id=1, source_target_pairs={{0,1008},{32,16},{64,48},{96,80},{128,112},{160,144},{192,176},{22... | collective-permute-start | bytes 196616 | tf_op jit(solution)/shard_map/ppermute | solution.py:214
  28.0 9.5 %collective-permute-start.1 = (f32[128,128]{1,0:T(8,128)S(1)}, f32[128,128]{1,0:T(8,128)S(1)}, u32[]{:S(2)}, u32[]{:S(2)}) collective-permute-start(f32[128,128]{1,0:T(8,128)S(1)} %fusion.9), channel_id=1, source_target_pairs={{0,16},{32,48},{64,80},{96,112},{128,144},{160,176},{192,208},{224... | collective-permute-start | bytes 196616 | tf_op jit(solution)/shard_map/ppermute | solution.py:212
  38.0 3.2 %collective-permute-start.3 = (f32[128,128]{1,0:T(8,128)S(1)}, f32[128,128]{1,0:T(8,128)S(1)}, u32[]{:S(2)}, u32[]{:S(2)}) collective-permute-start(f32[128,128]{1,0:T(8,128)S(1)} %fusion.11), channel_id=1, source_target_pairs={{16,32},{48,64},{80,96},{112,128},{144,160},{176,192},{208,224},{2... | collective-permute-start | bytes 196616 | tf_op jit(solution)/shard_map/ppermute | solution.py:216
  64.7 14.9 %collective-permute-start.4 = (f32[576,128]{1,0:T(8,128)}, f32[576,128]{1,0:T(8,128)S(1)}, u32[]{:S(2)}, u32[]{:S(2)}) collective-permute-start(f32[576,128]{1,0:T(8,128)} %get-tuple-element.11), channel_id=1, source_target_pairs={{0,16},{16,0},{1,17},{17,1},{2,18},{18,2},{3,19},{19,3},{4,20},{20... | collective-permute-start | bytes 884744 | tf_op jit(solution)/shard_map/ppermute | solution.py:50
  183.7 15.6 %copy-start.3 = (f32[8,72,128]{2,1,0:T(8,128)}, f32[8,72,128]{2,1,0:T(8,128)S(1)}, u32[]{:S(2)}) copy-start(f32[8,72,128]{2,1,0:T(8,128)S(1)} %all_to_all.27) | copy-start | bytes 884740
  184.6 21.5 %all-to-all-start.4 = ((f32[16,64,128]{2,1,0:T(8,128)}), f32[16,64,128]{2,1,0:T(8,128)S(1)}, u32[]{:S(2)}, u32[]{:S(2)}) async-start(f32[16,64,128]{2,1,0:T(8,128)} %broadcast_in_dim.20), calls=%async_computation.4 | async-start | bytes 1048576 | tf_op jit(solution)/shard_map/all_to_all | solution.py:46
  189.0 10.2 %collective-permute-start.5 = (f32[576,128]{1,0:T(8,128)S(1)}, f32[576,128]{1,0:T(8,128)S(1)}, u32[]{:S(2)}, u32[]{:S(2)}) collective-permute-start(f32[576,128]{1,0:T(8,128)S(1)} %bitcast.27), channel_id=1, source_target_pairs={{0,16},{16,0},{1,17},{17,1},{2,18},{18,2},{3,19},{19,3},{4,20},{20... | collective-permute-start | bytes 884744 | tf_op jit(solution)/shard_map/ppermute | solution.py:50
  199.3 0.7 copy-start.5
  206.2 0.8 copy-start.4
  209.4 3.6 %collective-permute-start.6 = (f32[512,128]{1,0:T(8,128)}, f32[512,128]{1,0:T(8,128)S(1)}, u32[]{:S(2)}, u32[]{:S(2)}) collective-permute-start(f32[512,128]{1,0:T(8,128)} %couple.1.refs_0_), channel_id=1, source_target_pairs={{0,16},{16,0},{1,17},{17,1},{2,18},{18,2},{3,19},{19,3},{4,20},{20... | collective-permute-start | bytes 786440 | tf_op jit(solution)/shard_map/ppermute | solution.py:50
  213.0 0.7 copy-start.6

commit v3 on v2

--- a/solution.py
+++ b/solution.py
@@ -26,19 +26,16 @@
     return lax.dot_general(left, right, (((1,), (1,)), ((), ())), precision=HIGHEST, preferred_element_type=F32)
 
 
-def store_thirds(target, array):
+def store_pieces(target, array):
     width = array.shape[1]
     high = array.astype(BF16)
-    rest = array - high.astype(F32)
-    mid = rest.astype(BF16)
     target[:, :width] = high
-    target[:, width : 2 * width] = mid
-    target[:, 2 * width :] = (rest - mid.astype(F32)).astype(BF16)
+    target[:, width:] = (array - high.astype(F32)).astype(BF16)
 
 
 def fold(wide):
-    width = wide.shape[1] // 3
-    return wide[:, :width] + (wide[:, width : 2 * width] + wide[:, 2 * width :])
+    width = wide.shape[1] // 2
+    return wide[:, :width] + wide[:, width:]
 
 
 def to_everyone(array, axis):
@@ -50,13 +47,32 @@
     return lax.ppermute(array, "core", [(0, 1), (1, 0)])
 
 
+def copies_kernel(source_ref, out_ref, sems):
+    moves = [pltpu.make_async_copy(source_ref, out_ref.at[i], sems.at[i]) for i in range(out_ref.shape[0])]
+    for move in moves:
+        move.start()
+    for move in moves:
+        move.wait()
+
+
+def copies(array, count):
+    return pl.pallas_call(
+        copies_kernel,
+        out_shape=jax.ShapeDtypeStruct((count, *array.shape), array.dtype),
+        in_specs=[pl.BlockSpec(memory_space=pltpu.VMEM)],
+        out_specs=pl.BlockSpec(memory_space=pl.ANY),
+        scratch_shapes=[pltpu.SemaphoreType.DMA((count,))],
+        name="copies",
+    )(array)
+
+
 def project_kernel(core_ref, panel_ref, own_ref, current_ref, send_ref, keep_ref, split):
     del core_ref
     step = pl.program_id(0)
 
     @pl.when(step == 0)
     def _():
-        store_thirds(split, current_ref[...])
+        store_pieces(split, current_ref[...])
 
     rows = panel_ref.shape[0] * panel_ref.shape[1]
     own, width = own_ref.shape[0], current_ref.shape[1]
@@ -83,7 +99,7 @@
     rows, width = sources // 2 * own, current.shape[1]
     total = 2 * rows + own * (rows // width)
     whole = pl.BlockSpec((total, width), lambda i, c: (0, 0))
-    flops = 2 * 2 * sources * own * depth_rows * width * 3
+    flops = 2 * 2 * sources * own * depth_rows * width * 2
     return pl.pallas_call(
         project_kernel,
         out_shape=[jax.ShapeDtypeStruct((total, width), F32)] * 2,
@@ -99,72 +115,133 @@
                 pl.BlockSpec(current.shape, lambda i, c: (0, 0)),
             ],
             out_specs=[whole, whole],
-            scratch_shapes=[pltpu.VMEM((depth_rows, 3 * width), BF16)],
+            scratch_shapes=[pltpu.VMEM((depth_rows, 2 * width), BF16)],
         ),
         cost_estimate=pl.CostEstimate(flops=flops, bytes_accessed=panels.size * 2 + current.size * 4, transcendentals=0),
         name="project",
     )(core, panels, panel_vectors, current)
 
 
-def apply_kernel(first_row, corrections, core_ref, mine_ref, other_ref, factor_ref, panel_ref, current_ref, *refs):
-    correction_refs, (weights_ref, out_ref, total, split) = refs[:corrections], refs[corrections:]
+def weigh(first_row, core_ref, mine_ref, other_ref, factor_ref, total, corrections=()):
     depth = factor_ref.shape[0]
     half = depth // 2
-
+    for which, (low_ref, high_ref) in enumerate(((mine_ref, other_ref), (other_ref, mine_ref))):
+
+        @pl.when(core_ref[0] == which)
+        def _(low_ref=low_ref, high_ref=high_ref):
+            total[:half] = low_ref[first_row : first_row + half]
+            total[half:] = high_ref[first_row : first_row + half]
+
+    wanted = total[...]
+    if corrections:
+        wanted = wanted - (corrections[0][...] + corrections[1][...])
+    row = lax.broadcasted_iota(jnp.int32, (depth, depth), 0)
+    column = lax.broadcasted_iota(jnp.int32, (depth, depth), 1)
+    return product(jnp.where(row <= column, factor_ref[...], 0.0), wanted)
+
+
+def first_weights_kernel(core_ref, mine_ref, other_ref, factor_ref, weights_ref, total):
+    weights_ref[...] = weigh(0, core_ref, mine_ref, other_ref, factor_ref, total)
+
+
+def first_weights(core, mine, other, panel_factor):
+    depth, width = panel_factor.shape[1], mine.shape[1]
+    whole = pl.BlockSpec(mine.shape, lambda i, c: (0, 0))
+    return pl.pallas_call(
+        first_weights_kernel,
+        out_shape=jax.ShapeDtypeStruct((depth, width), F32),
+        grid_spec=pltpu.PrefetchScalarGridSpec(
+            num_scalar_prefetch=1,
+            grid=(1,),
+            in_specs=[whole, whole, pl.BlockSpec((None, depth, depth), lambda i, c: (0, 0, 0))],
+            out_specs=pl.BlockSpec((depth, width), lambda i, c: (0, 0)),
+            scratch_shapes=[pltpu.VMEM((depth, width), F32)],
+        ),
+        cost_estimate=pl.CostEstimate(flops=2 * depth * depth * width * 6, bytes_accessed=4 * depth * depth, transcendentals=0),
+        name="first_weights",
+    )(core, mine, other, panel_factor)
+
+
+def update(panel_ref, split, current_ref, out_ref):
+    panel = panel_ref[...].reshape(split.shape[0], panel_ref.shape[2])
+    wide = lax.dot_general(panel, split[...], (((0,), (0,)), ((), ())), preferred_element_type=F32)
+    out_ref[...] = current_ref[...] - fold(wide)
+
+
+def apply_kernel(weights_ref, panel_ref, current_ref, out_ref, split):
     @pl.when(pl.program_id(0) == 0)
     def _():
-        for which, (low_ref, high_ref) in enumerate(((mine_ref, other_ref), (other_ref, mine_ref))):
-
-            @pl.when(core_ref[0] == which)
-            def _(low_ref=low_ref, high_ref=high_ref):
-                total[:half] = low_ref[first_row : first_row + half]
-                total[half:] = high_ref[first_row : first_row + half]
-
-        wanted = total[...]
-        if corrections:
-            wanted = wanted - (correction_refs[0][...] + correction_refs[1][...])
-        row = lax.broadcasted_iota(jnp.int32, (depth, depth), 0)
-        column = lax.broadcasted_iota(jnp.int32, (depth, depth), 1)
-        factor = jnp.where(row <= column, factor_ref[...], 0.0)
-        weights = product(factor, wanted)
-        weights_ref[...] = weights
-        store_thirds(split, weights)
-
-    panel = panel_ref[...].reshape(depth, panel_ref.shape[2])
-    update = lax.dot_general(panel, split[...], (((0,), (0,)), ((), ())), preferred_element_type=F32)
-    out_ref[...] = current_ref[...] - fold(update)
-
-
-def apply_panel(core, mine, other, panel_factor, panels, current, index, first_row, corrections=()):
+        store_pieces(split, weights_ref[...])
+
+    update(panel_ref, split, current_ref, out_ref)
+
+
+STEPS = 4
+
+
+def apply_first(weights, panels, current):
     sources, _, own, n_rows = panels.shape
-    depth, width = panel_factor.shape[1], current.shape[1]
-    steps = 4
-    block = n_rows // steps
+    depth, width = weights.shape
+    block = n_rows // STEPS
+    rows = pl.BlockSpec((block, width), lambda i: (i, 0))
+    return pl.pallas_call(
+        apply_kernel,
+        out_shape=jax.ShapeDtypeStruct(current.shape, F32),
+        grid=(STEPS,),
+        in_specs=[
+            pl.BlockSpec((depth, width), lambda i: (0, 0)),
+            pl.BlockSpec((sources, None, own, block), lambda i: (0, 0, 0, i)),
+            rows,
+        ],
+        out_specs=rows,
+        scratch_shapes=[pltpu.VMEM((depth, 2 * width), BF16)],
+        cost_estimate=pl.CostEstimate(
+            flops=2 * n_rows * depth * width * 2, bytes_accessed=panels.size + current.size * 8, transcendentals=0
+        ),
+        name="apply_first",
+    )(weights, panels, current)
+
+
+def finish_kernel(
+    first_row, core_ref, mine_ref, other_ref, factor_ref, own_part, other_part, panel_ref, current_ref, out_ref, total, split
+):
+    @pl.when(pl.program_id(0) == 0)
+    def _():
+        store_pieces(
+            split, weigh(first_row, core_ref, mine_ref, other_ref, factor_ref, total, (own_part, other_part))
+        )
+
+    update(panel_ref, split, current_ref, out_ref)
+
+
+def finish(core, mine, other, panel_factor, own_part, other_part, panels, current, first_row):
+    sources, _, own, n_rows = panels.shape
+    depth, width = own_part.shape
+    block = n_rows // STEPS
     whole = lambda array: pl.BlockSpec(array.shape, lambda i, c: (0, 0))
-    flops = 2 * n_rows * depth * width * 3 + 2 * depth * depth * width * 6
-    return pl.pallas_call(
-        functools.partial(apply_kernel, first_row, len(corrections)),
-        out_shape=[jax.ShapeDtypeStruct((depth, width), F32), jax.ShapeDtypeStruct(current.shape, F32)],
+    rows = pl.BlockSpec((block, width), lambda i, c: (i, 0))
+    flops = 2 * n_rows * depth * width * 2 + 2 * depth * depth * width * 6
+    return pl.pallas_call(
+        functools.partial(finish_kernel, first_row),
+        out_shape=jax.ShapeDtypeStruct(current.shape, F32),
         grid_spec=pltpu.PrefetchScalarGridSpec(
             num_scalar_prefetch=1,
-            grid=(steps,),
+            grid=(STEPS,),
             in_specs=[
                 whole(mine),
                 whole(other),
-                pl.BlockSpec((None, depth, depth), lambda i, c: (index, 0, 0)),
-                pl.BlockSpec((sources, None, own, block), lambda i, c: (0, index, 0, i)),
-                pl.BlockSpec((block, width), lambda i, c: (i, 0)),
-                *[whole(array) for array in corrections],
+                pl.BlockSpec((None, depth, depth), lambda i, c: (1, 0, 0)),
+                whole(own_part),
+                whole(other_part),
+                pl.BlockSpec((sources, None, own, block), lambda i, c: (0, 1, 0, i)),
+                rows,
             ],
-            out_specs=[
-                pl.BlockSpec((depth, width), lambda i, c: (0, 0)),
-                pl.BlockSpec((block, width), lambda i, c: (i, 0)),
-            ],
-            scratch_shapes=[pltpu.VMEM((depth, width), F32), pltpu.VMEM((depth, 3 * width), BF16)],
+            out_specs=rows,
+            scratch_shapes=[pltpu.VMEM((depth, width), F32), pltpu.VMEM((depth, 2 * width), BF16)],
         ),
         cost_estimate=pl.CostEstimate(flops=flops, bytes_accessed=panels.size + current.size * 8, transcendentals=0),
-        name="apply_panel",
-    )(core, mine, other, panel_factor, panels, current, *corrections)
+        name="finish",
+    )(core, mine, other, panel_factor, own_part, other_part, panels, current)
 
 
 def couple_kernel(core_ref, gram_ref, weights_ref, out_ref):
@@ -201,7 +278,8 @@
     core = core_index.astype(jnp.int32).reshape(1)
     n = lax.axis_size(ROW)
 
-    panels = to_everyone(panel_vectors, "vec")
+    panel_copies = copies(panel_vectors, lax.axis_size("vec"))
+    panels = lax.all_to_all(panel_copies, "vec", split_axis=0, concat_axis=0, tiled=True)
 
     factor = jnp.triu(band_factor[0])
     own = product(band_head, vectors)
@@ -231,11 +309,10 @@
     gram = to_everyone(mine[half:gram_end], "vec")
     other = swapped(mine)
 
-    weights0, current = apply_panel(core, mine, other, panel_factor, panels, current, 0, 0)
+    weights0 = first_weights(core, mine, other, panel_factor)
     coupled = couple(core, gram, weights0)
-    corrections = (coupled, swapped(coupled))
-    _, result = apply_panel(core, mine, other, panel_factor, panels, current, 1, gram_end, corrections)
-    return result
+    current = apply_first(weights0, panels, current)
+    return finish(core, mine, other, panel_factor, coupled, swapped(coupled), panels, current, gram_end)
 
 
 def solution(mesh):

time: 221 us -> 222 us (level)
  local copies, waits for them, and re-layouts: 6.76 us -> 3.24 us
  Pallas kernels: 21.9 us -> 25.3 us
  starting transfers between devices: 53.8 us -> 56.6 us
    all_to_all x0 -> x1, waiting for transfers between devices: none -> 15 us  [on_device(): lax.all_to_all(panel_copies, 'vec', split_axis=0, concat_axis=0, tiled=True)]
    all_to_all x2 -> x1, waiting for transfers between devices: 15 us -> 0.01 us  [to_everyone(): return lax.all_to_all(copies, axis, split_axis=0, concat_axis=0, tiled=True)]
    all_to_all x0 -> x1, starting transfers between devices: none -> 7.77 us  [on_device(): lax.all_to_all(panel_copies, 'vec', split_axis=0, concat_axis=0, tiled=True)]
    all_to_all x2 -> x1, starting transfers between devices: 12.1 us -> 4.39 us  [to_everyone(): return lax.all_to_all(copies, axis, split_axis=0, concat_axis=0, tiled=True)]
    pallas_call x2 -> x4, Pallas kernels: 12.5 us -> 16.9 us  [the longest x1 6.08 us: finish(): pl.pallas_call(functools.partial(finish_kernel, first_row), out_shape=jax...]
    broadcast_in_dim x4 -> x3, local copies, waits for them, and re-layouts: 4.47 us -> 0.92 us  [to_everyone(): copies = jnp.broadcast_to(array, (lax.axis_size(axis), *array.shape))]
    ppermute x3, starting transfers between devices: 24.9 us -> 27.6 us  [swapped(): return lax.ppermute(array, 'core', [(0, 1), (1, 0)])]
  transfers between devices with their start and end apart: 9 -> 9, of which waited for: 6 -> 5; matrix products, arithmetic and copies ran while one was open for 3% -> 3% of each run, Pallas kernels for 3% -> 3%
where the time goes in v3:
time: 222 us; the launch traced here: 221 us
  blocking collectives  103 us (46%)
  starting transfers between devices  56.6 us (25%)
  waiting for transfers between devices  25.7 us (12%)
  Pallas kernels  25.3 us (11%)
  matrix products  5.29 us (2%)
  local copies, waits for them, and re-layouts  3.24 us (1%)
    all_to_all x2, blocking collectives, to_everyone(): return lax.all_to_all(copies, axis, split_axis=0, concat_axis=0, tiled=True)  66.6 us
    all_to_all x1, blocking collectives, on_device(): lax.all_to_all(blocks, 'near', split_axis=0, concat_axis=0, tiled=True)  36.3 us
    ppermute x3, starting transfers between devices, swapped(): return lax.ppermute(array, 'core', [(0, 1), (1, 0)])  27.6 us
    all_to_all x1, waiting for transfers between devices, on_device(): lax.all_to_all(panel_copies, 'vec', split_axis=0, concat_axis=0, tiled=True)  15 us
    ppermute x1, starting transfers between devices, on_device(): tail_next = lax.ppermute(tail, ROW, [(i + 1, i) for i in range(0, n, 2)])  12.9 us
    all_to_all x1, starting transfers between devices, on_device(): lax.all_to_all(panel_copies, 'vec', split_axis=0, concat_axis=0, tiled=True)  7.77 us
    pallas_call x1, Pallas kernels, finish(): pl.pallas_call(functools.partial(finish_kernel, first_row), out_shape=jax...  6.08 us
    pallas_call x1, Pallas kernels, project(): pl.pallas_call(project_kernel, out_shape=[jax.ShapeDtypeStruct((total, wi...  5.98 us
  transfers between devices with their start and end apart: 9, of which 5 were waited for; matrix products, arithmetic and copies ran while one was open for 3% of the time, Pallas kernels for 3%

profile of v3, /device:TPU:1, one launch (start us, length us, event | category | flops | bytes accessed | tf_op | source)
XLA Modules:
  0.0 221.4 jit_solution(16100564288172270)
XLA Ops:
  0.0 3.1 %copies.1 = bf16[16,2,32,2048]{3,2,1,0:T(8,128)(2,1)} custom-call(bf16[2,32,2048]{2,1,0:T(8,128)(2,1)} %own_ref.1), custom_call_target="tpu_custom_call" | custom-call | tf_op jit(solution)/shard_map/copies/pallas_call | solution.py:59
  3.2 7.8 %all-to-all-start = ((bf16[16,2,32,2048]{3,2,1,0:T(8,128)(2,1)}), bf16[16,2,32,2048]{3,2,1,0:T(8,128)(2,1)}, u32[]{:S(2)}, u32[]{:S(2)}) async-start(bf16[16,2,32,2048]{3,2,1,0:T(8,128)(2,1)} %copies.1), calls=%async_computation | async-start | bytes 8388608 | tf_op jit(solution)/shard_map/all_to_all | solution.py:282
  11.3 12.9 %collective-permute-start = (f32[128,128]{1,0:T(8,128)S(1)}, f32[128,128]{1,0:T(8,128)S(1)}, u32[]{:S(2)}, u32[]{:S(2)}) collective-permute-start(f32[128,128]{1,0:T(8,128)S(1)} %fusion.5), channel_id=1, source_target_pairs={{16,0},{48,32},{80,64},{112,96},{144,128},{176,160},{208,192},{240... | collective-permute-start | bytes 196616 | tf_op jit(solution)/shard_map/ppermute | solution.py:288
  26.3 1.3 collective-permute-start.2
  27.6 1.3 collective-permute-start.1
  28.9 3.4 %collective-permute-done.2 = f32[128,128]{1,0:T(8,128)S(1)} collective-permute-done((f32[128,128]{1,0:T(8,128)S(1)}, f32[128,128]{1,0:T(8,128)S(1)}, u32[]{:S(2)}, u32[]{:S(2)}) %collective-permute-start.2) | collective-permute-done | bytes 65568 | tf_op jit(solution)/shard_map/ppermute | solution.py:292
  32.3 4.8 %collective-permute-done.1 = f32[128,128]{1,0:T(8,128)S(1)} collective-permute-done((f32[128,128]{1,0:T(8,128)S(1)}, f32[128,128]{1,0:T(8,128)S(1)}, u32[]{:S(2)}, u32[]{:S(2)}) %collective-permute-start.1) | collective-permute-done | bytes 65568 | tf_op jit(solution)/shard_map/ppermute | solution.py:290
  37.6 1.3 collective-permute-start.3
  38.9 1.8 fusion
  42.5 15.0 %all-to-all-done.panel_ref = bf16[16,2,32,2048]{3,2,1,0:T(8,128)(2,1)} async-done(((bf16[16,2,32,2048]{3,2,1,0:T(8,128)(2,1)}), bf16[16,2,32,2048]{3,2,1,0:T(8,128)(2,1)}, u32[]{:S(2)}, u32[]{:S(2)}) %all-to-all-start) | async-done | bytes 4194336 | tf_op jit(solution)/shard_map/all_to_all | solution.py:282
  57.4 6.0 %project.1 = (f32[576,128]{1,0:T(8,128)}, f32[576,128]{1,0:T(8,128)}) custom-call(s32[1]{0:T(128)} %bitcast.core_ref, bf16[16,2,32,2048]{3,2,1,0:T(8,128)(2,1)} %all-to-all-done.panel_ref, bf16[2,32,2048]{2,1,0:T(8,128)(2,1)} %own_ref.1, f32[2048,128]{1,0:T(8,128)} %pad_maximum_fusion.current_ref), custom_call_target="tpu_custom_call" | custom-call | flops 1073741824 | bytes 5242880 | tf_op jit(solution)/shard_map/project/pallas_call | solution.py:103
  63.4 13.5 %collective-permute-start.4 = (f32[576,128]{1,0:T(8,128)}, f32[576,128]{1,0:T(8,128)S(1)}, u32[]{:S(2)}, u32[]{:S(2)}) collective-permute-start(f32[576,128]{1,0:T(8,128)} %get-tuple-element.8), channel_id=1, source_target_pairs={{0,16},{16,0},{1,17},{17,1},{2,18},{18,2},{3,19},{19,3},{4,20},{20... | collective-permute-start | bytes 884744 | tf_op jit(solution)/shard_map/ppermute | solution.py:47
  76.9 1.4 collective-permute-done.4
  79.3 36.3 %all_to_all.25 = f32[8,72,128]{2,1,0:T(8,128)S(1)} all-to-all(f32[8,72,128]{2,1,0:T(8,128)S(1)} %bitcast.30), channel_id=1, replica_groups=mesh['far'=4,'near'=8,'core'=2,'vec'=16] {'near'}, dimensions={0} | all-to-all | bytes 589824 | tf_op jit(solution)/shard_map/all_to_all | solution.py:304
  115.7 42.1 %all_to_all.26 = f32[4,72,128]{2,1,0:T(8,128)S(1)} all-to-all(f32[4,72,128]{2,1,0:T(8,128)S(1)} %broadcast_in_dim.14), channel_id=1, replica_groups=mesh['far'=4,'near'=8,'core'=2,'vec'=16] {'far'}, dimensions={0} | all-to-all | bytes 294912 | tf_op jit(solution)/shard_map/all_to_all | solution.py:43
  157.9 24.5 %all_to_all.27 = f32[8,72,128]{2,1,0:T(8,128)S(1)} all-to-all(f32[8,72,128]{2,1,0:T(8,128)S(1)} %broadcast_in_dim.15), channel_id=1, replica_groups=mesh['far'=4,'near'=8,'core'=2,'vec'=16] {'near'}, dimensions={0} | all-to-all | bytes 589824 | tf_op jit(solution)/shard_map/all_to_all | solution.py:43
  183.3 4.4 %all-to-all-start.4 = ((f32[16,64,128]{2,1,0:T(8,128)}), f32[16,64,128]{2,1,0:T(8,128)S(1)}, u32[]{:S(2)}, u32[]{:S(2)}) async-start(f32[16,64,128]{2,1,0:T(8,128)} %broadcast_in_dim.16), calls=%async_computation.4 | async-start | bytes 1048576 | tf_op jit(solution)/shard_map/all_to_all | solution.py:43
  187.7 9.0 %collective-permute-start.5 = (f32[576,128]{1,0:T(8,128)S(1)}, f32[576,128]{1,0:T(8,128)S(1)}, u32[]{:S(2)}, u32[]{:S(2)}) collective-permute-start(f32[576,128]{1,0:T(8,128)S(1)} %bitcast.27), channel_id=1, source_target_pairs={{0,16},{16,0},{1,17},{17,1},{2,18},{18,2},{3,19},{19,3},{4,20},{20... | collective-permute-start | bytes 884744 | tf_op jit(solution)/shard_map/ppermute | solution.py:47
  196.7 1.2 collective-permute-done.5.other_ref
  198.6 3.1 %first_weights.1.weights_ref = f32[512,128]{1,0:T(8,128)} custom-call(s32[1]{0:T(128)} %bitcast.core_ref, f32[576,128]{1,0:T(8,128)} %bitcast.28, f32[576,128]{1,0:T(8,128)} %copy-done.5, f32[2,512,512]{2,1,0:T(8,128)} %factor_ref.3), custom_call_target="tpu_custom_call" | custom-call | flops 402653184 | bytes 1048576 | tf_op jit(solution)/shard_map/first_weights/pallas_call | solution.py:150
  202.6 2.4 %couple.1.own_part = f32[512,128]{1,0:T(8,128)} custom-call(s32[1]{0:T(128)} %bitcast.core_ref, f32[16,64,128]{2,1,0:T(8,128)} %copy-done.4, f32[512,128]{1,0:T(8,128)} %first_weights.1.weights_ref), custom_call_target="tpu_custom_call" | custom-call | flops 201326592 | bytes 524288 | tf_op jit(solution)/shard_map/couple/pallas_call | solution.py:262
  205.0 5.1 %collective-permute-start.6 = (f32[512,128]{1,0:T(8,128)}, f32[512,128]{1,0:T(8,128)S(1)}, u32[]{:S(2)}, u32[]{:S(2)}) collective-permute-start(f32[512,128]{1,0:T(8,128)} %couple.1.own_part), channel_id=1, source_target_pairs={{0,16},{16,0},{1,17},{17,1},{2,18},{18,2},{3,19},{19,3},{4,20},{20... | collective-permute-start | bytes 786440 | tf_op jit(solution)/shard_map/ppermute | solution.py:47
  210.0 4.6 %apply_first.1.current_ref = f32[2048,128]{1,0:T(8,128)} custom-call(f32[512,128]{1,0:T(8,128)} %first_weights.1.weights_ref, bf16[16,2,32,2048]{3,2,1,0:T(8,128)(2,1)} %all-to-all-done.panel_ref, f32[2048,128]{1,0:T(8,128)} %pad_maximum_fusion.current_ref), custom_call_target="tpu_custom_call" | custom-call | flops 536870912 | bytes 4194304 | tf_op jit(solution)/shard_map/apply_first/pallas_call | solution.py:187
  215.3 6.1 %finish.1 = f32[2048,128]{1,0:T(8,128)} custom-call(s32[1]{0:T(128)} %bitcast.core_ref, f32[576,128]{1,0:T(8,128)} %bitcast.29, f32[576,128]{1,0:T(8,128)} %copy-done.5, f32[2,512,512]{2,1,0:T(8,128)} %factor_ref.3, f32[512,128]{1,0:T(8,128)} %couple.1.own_part, f32[512,128]{1,0:T(8,128)} %copy-done.6, bf16[16,2,32,2048]{3,2,1,0:T(8,128)(2,1)} %all-to-all-done.panel_ref, ...), custom_call_target="tpu_custom_call" | custom-call | flops 939524096 | bytes 4194304 | tf_op jit(solution)/shard_map/finish/pallas_call | solution.py:224
  (38 shorter events, 8.8 us)
Async XLA Ops:
  0.0 10.9 %copy-start = (f32[128,512]{1,0:T(8,128)S(1)}, f32[128,512]{1,0:T(8,128)}, u32[]{:S(2)}) copy-start(f32[128,512]{1,0:T(8,128)} %param.8) | copy-start | bytes 786436
  3.1 7.8 %copy-start.1 = (f32[2048,128]{1,0:T(8,128)S(1)}, f32[2048,128]{1,0:T(8,128)}, u32[]{:S(2)}) copy-start(f32[2048,128]{1,0:T(8,128)} %param.6) | copy-start | bytes 3145732
  3.1 21.2 %copy-start.2 = (f32[128,2048]{1,0:T(8,128)S(1)}, f32[128,2048]{1,0:T(8,128)}, u32[]{:S(2)}) copy-start(f32[128,2048]{1,0:T(8,128)} %param.7) | copy-start | bytes 3145732
  3.1 22.7 %copy-start.7 = (f32[1,128,128]{2,1,0:T(8,128)S(1)}, f32[1,128,128]{2,1,0:T(8,128)}, u32[]{:S(2)}) copy-start(f32[1,128,128]{2,1,0:T(8,128)} %param.9) | copy-start | bytes 196612
  3.2 54.3 %all-to-all-start = ((bf16[16,2,32,2048]{3,2,1,0:T(8,128)(2,1)}), bf16[16,2,32,2048]{3,2,1,0:T(8,128)(2,1)}, u32[]{:S(2)}, u32[]{:S(2)}) async-start(bf16[16,2,32,2048]{3,2,1,0:T(8,128)(2,1)} %copies.1), calls=%async_computation | async-start | bytes 8388608 | tf_op jit(solution)/shard_map/all_to_all | solution.py:282
  11.3 14.5 %collective-permute-start = (f32[128,128]{1,0:T(8,128)S(1)}, f32[128,128]{1,0:T(8,128)S(1)}, u32[]{:S(2)}, u32[]{:S(2)}) collective-permute-start(f32[128,128]{1,0:T(8,128)S(1)} %fusion.5), channel_id=1, source_target_pairs={{16,0},{48,32},{80,64},{112,96},{144,128},{176,160},{208,192},{240... | collective-permute-start | bytes 196616 | tf_op jit(solution)/shard_map/ppermute | solution.py:288
  26.3 6.0 %collective-permute-start.2 = (f32[128,128]{1,0:T(8,128)S(1)}, f32[128,128]{1,0:T(8,128)S(1)}, u32[]{:S(2)}, u32[]{:S(2)}) collective-permute-start(f32[128,128]{1,0:T(8,128)S(1)} %convolution_subtract_fusion), channel_id=1, source_target_pairs={{0,1008},{32,16},{64,48},{96,80},{128,112},{160,144},{192,176},{22... | collective-permute-start | bytes 196616 | tf_op jit(solution)/shard_map/ppermute | solution.py:292
  27.6 9.4 %collective-permute-start.1 = (f32[128,128]{1,0:T(8,128)S(1)}, f32[128,128]{1,0:T(8,128)S(1)}, u32[]{:S(2)}, u32[]{:S(2)}) collective-permute-start(f32[128,128]{1,0:T(8,128)S(1)} %fusion.9), channel_id=1, source_target_pairs={{0,16},{32,48},{64,80},{96,112},{128,144},{160,176},{192,208},{224... | collective-permute-start | bytes 196616 | tf_op jit(solution)/shard_map/ppermute | solution.py:290
  37.6 3.2 %collective-permute-start.3 = (f32[128,128]{1,0:T(8,128)S(1)}, f32[128,128]{1,0:T(8,128)S(1)}, u32[]{:S(2)}, u32[]{:S(2)}) collective-permute-start(f32[128,128]{1,0:T(8,128)S(1)} %fusion.11), channel_id=1, source_target_pairs={{16,32},{48,64},{80,96},{112,128},{144,160},{176,192},{208,224},{2... | collective-permute-start | bytes 196616 | tf_op jit(solution)/shard_map/ppermute | solution.py:294
  63.4 14.9 %collective-permute-start.4 = (f32[576,128]{1,0:T(8,128)}, f32[576,128]{1,0:T(8,128)S(1)}, u32[]{:S(2)}, u32[]{:S(2)}) collective-permute-start(f32[576,128]{1,0:T(8,128)} %get-tuple-element.8), channel_id=1, source_target_pairs={{0,16},{16,0},{1,17},{17,1},{2,18},{18,2},{3,19},{19,3},{4,20},{20... | collective-permute-start | bytes 884744 | tf_op jit(solution)/shard_map/ppermute | solution.py:47
  182.4 15.5 %copy-start.3 = (f32[8,72,128]{2,1,0:T(8,128)}, f32[8,72,128]{2,1,0:T(8,128)S(1)}, u32[]{:S(2)}) copy-start(f32[8,72,128]{2,1,0:T(8,128)S(1)} %all_to_all.27) | copy-start | bytes 884740
  183.3 18.5 %all-to-all-start.4 = ((f32[16,64,128]{2,1,0:T(8,128)}), f32[16,64,128]{2,1,0:T(8,128)S(1)}, u32[]{:S(2)}, u32[]{:S(2)}) async-start(f32[16,64,128]{2,1,0:T(8,128)} %broadcast_in_dim.16), calls=%async_computation.4 | async-start | bytes 1048576 | tf_op jit(solution)/shard_map/all_to_all | solution.py:43
  187.7 10.2 %collective-permute-start.5 = (f32[576,128]{1,0:T(8,128)S(1)}, f32[576,128]{1,0:T(8,128)S(1)}, u32[]{:S(2)}, u32[]{:S(2)}) collective-permute-start(f32[576,128]{1,0:T(8,128)S(1)} %bitcast.27), channel_id=1, source_target_pairs={{0,16},{16,0},{1,17},{17,1},{2,18},{18,2},{3,19},{19,3},{4,20},{20... | collective-permute-start | bytes 884744 | tf_op jit(solution)/shard_map/ppermute | solution.py:47
  197.9 0.7 copy-start.5
  201.8 0.8 copy-start.4
  205.0 9.6 %collective-permute-start.6 = (f32[512,128]{1,0:T(8,128)}, f32[512,128]{1,0:T(8,128)S(1)}, u32[]{:S(2)}, u32[]{:S(2)}) collective-permute-start(f32[512,128]{1,0:T(8,128)} %couple.1.own_part), channel_id=1, source_target_pairs={{0,16},{16,0},{1,17},{17,1},{2,18},{18,2},{3,19},{19,3},{4,20},{20... | collective-permute-start | bytes 786440 | tf_op jit(solution)/shard_map/ppermute | solution.py:47
  214.6 0.7 copy-start.6

commit v4 on v3

v4 whole, which is shorter than its diff:
```python
import functools

import jax
import jax.numpy as jnp
from jax import lax
from jax.experimental import pallas as pl
from jax.experimental.pallas import tpu as pltpu
from jax.sharding import Mesh
from jax.sharding import PartitionSpec as P

HIGHEST = lax.Precision.HIGHEST
F32 = jnp.float32
BF16 = jnp.bfloat16


def product(left, right):
    return jnp.dot(left, right, precision=HIGHEST, preferred_element_type=F32)


def product_t(left, right):
    return lax.dot_general(left, right, (((0,), (0,)), ((), ())), precision=HIGHEST, preferred_element_type=F32)


def product_nt(left, right):
    return lax.dot_general(left, right, (((1,), (1,)), ((), ())), precision=HIGHEST, preferred_element_type=F32)


def store_pieces(target, array):
    width = array.shape[1]
    high = array.astype(BF16)
    target[:, :width] = high
    target[:, width:] = (array - high.astype(F32)).astype(BF16)


def fold(wide):
    width = wide.shape[1] // 2
    return wide[:, :width] + wide[:, width:]


def exchanged(blocks, axis, groups=None):
    return lax.all_to_all(blocks, axis, split_axis=0, concat_axis=0, tiled=True, axis_index_groups=groups)


def to_everyone(array, axis, groups=None):
    members = lax.axis_size(axis) if groups is None else len(groups[0])
    return exchanged(jnp.broadcast_to(array, (members, *array.shape)), axis, groups)


def swapped(array):
    return lax.ppermute(array, "row", [(i, i ^ 1) for i in range(lax.axis_size("row"))])


def row_groups(devices):
    chips = devices // 2
    far = min(4, chips // 2)
    near = chips // far
    at = lambda core, f, p: 2 * ((near * f + near // 2 * core + p) % chips) + core
    near_groups = [[at(core, f, p) for p in range(near)] for core in range(2) for f in range(far)]
    far_groups = [[at(core, f, p) for f in range(far)] for core in range(2) for p in range(near)]
    return near_groups, far_groups


def copies_kernel(source_ref, out_ref, sems):
    moves = [pltpu.make_async_copy(source_ref, out_ref.at[i], sems.at[i]) for i in range(out_ref.shape[0])]
    for move in moves:
        move.start()
    for move in moves:
        move.wait()


def copies(array, count):
    return pl.pallas_call(
        copies_kernel,
        out_shape=jax.ShapeDtypeStruct((count, *array.shape), array.dtype),
        in_specs=[pl.BlockSpec(memory_space=pltpu.VMEM)],
        out_specs=pl.BlockSpec(memory_space=pl.ANY),
        scratch_shapes=[pltpu.SemaphoreType.DMA((count,))],
        name="copies",
    )(array)


def project_kernel(core_ref, panel_ref, own_ref, current_ref, after_ref, send_ref, keep_ref, split):
    del core_ref, after_ref
    step = pl.program_id(0)

    @pl.when(step == 0)
    def _():
        store_pieces(split, current_ref[...])

    rows = panel_ref.shape[0] * panel_ref.shape[1]
    own, width = own_ref.shape[0], current_ref.shape[1]
    tiles = rows // width
    gram_end = rows + own * tiles
    panel = panel_ref[...].reshape(rows, panel_ref.shape[2])
    part = fold(jnp.dot(panel, split[...], preferred_element_type=F32))
    for which, out_ref in enumerate((send_ref, keep_ref)):

        @pl.when(step == 2 * which)
        def _(out_ref=out_ref):
            out_ref[:rows] = part
            gram = lax.dot_general(own_ref[...], panel, (((1,), (1,)), ((), ())), preferred_element_type=F32)
            for t in range(tiles):
                out_ref[rows + own * t : rows + own * (t + 1)] = gram[:, width * t : width * (t + 1)]

        @pl.when(step == 2 * which + 1)
        def _(out_ref=out_ref):
            out_ref[gram_end:] = part


def project(core, panels, panel_vectors, current, after):
    sources, _, own, depth_rows = panels.shape
    rows, width = sources // 2 * own, current.shape[1]
    total = 2 * rows + own * (rows // width)
    whole = pl.BlockSpec((total, width), lambda i, c: (0, 0))
    flops = 2 * 2 * sources * own * depth_rows * width * 2
    return pl.pallas_call(
        project_kernel,
        out_shape=[jax.ShapeDtypeStruct((total, width), F32)] * 2,
        grid_spec=pltpu.PrefetchScalarGridSpec(
            num_scalar_prefetch=1,
            grid=(4,),
            in_specs=[
                pl.BlockSpec(
                    (sources // 2, None, own, depth_rows),
                    lambda i, c: (jnp.where(i < 2, 1 - c[0], c[0]), i % 2, 0, 0),
                ),
                pl.BlockSpec((None, own, depth_rows), lambda i, c: (1, 0, 0)),
                pl.BlockSpec(current.shape, lambda i, c: (0, 0)),
                pl.BlockSpec(memory_space=pl.ANY),
            ],
            out_specs=[whole, whole],
            scratch_shapes=[pltpu.VMEM((depth_rows, 2 * width), BF16)],
        ),
        cost_estimate=pl.CostEstimate(flops=flops, bytes_accessed=panels.size * 2 + current.size * 4, transcendentals=0),
        name="project",
    )(core, panels, panel_vectors, current, after)


def prepare_kernel(factor_ref, out_ref):
    depth = factor_ref.shape[0]
    row = lax.broadcasted_iota(jnp.int32, (depth, depth), 0)
    column = lax.broadcasted_iota(jnp.int32, (depth, depth), 1)
    store_pieces(out_ref, jnp.where(row <= column, factor_ref[...], 0.0))


def prepare(panel_factor):
    count, depth, _ = panel_factor.shape
    return pl.pallas_call(
        prepare_kernel,
        out_shape=jax.ShapeDtypeStruct((count, depth, 2 * depth), BF16),
        grid=(count,),
        in_specs=[pl.BlockSpec((None, depth, depth), lambda i: (i, 0, 0))],
        out_specs=pl.BlockSpec((None, depth, 2 * depth), lambda i: (i, 0, 0)),
        cost_estimate=pl.CostEstimate(flops=panel_factor.size, bytes_accessed=panel_factor.size * 8, transcendentals=0),
        name="prepare",
    )(panel_factor)


def in_pieces(left_high, left_low, right):
    width = right.shape[1] // 2
    main = jnp.dot(left_high, right, preferred_element_type=F32)
    return fold(main) + jnp.dot(left_low, right[:, :width], preferred_element_type=F32)


def weigh(first_row, core_ref, mine_ref, other_ref, factor_ref, total, split, corrections=()):
    depth = factor_ref.shape[0]
    half = depth // 2
    for which, (low_ref, high_ref) in enumerate(((mine_ref, other_ref), (other_ref, mine_ref))):

        @pl.when(core_ref[0] == which)
        def _(low_ref=low_ref, high_ref=high_ref):
            total[:half] = low_ref[first_row : first_row + half]
            total[half:] = high_ref[first_row : first_row + half]

    wanted = total[...]
    if corrections:
        wanted = wanted - (corrections[0][...] + corrections[1][...])
    store_pieces(split, wanted)
    return in_pieces(factor_ref[:, :depth], factor_ref[:, depth:], split[...])


def first_weights_kernel(core_ref, mine_ref, other_ref, factor_ref, weights_ref, total, split):
    store_pieces(weights_ref, weigh(0, core_ref, mine_ref, other_ref, factor_ref, total, split))


def first_weights(core, mine, other, factors):
    depth, width = factors.shape[1], mine.shape[1]
    whole = pl.BlockSpec(mine.shape, lambda i, c: (0, 0))
    return pl.pallas_call(
        first_weights_kernel,
        out_shape=jax.ShapeDtypeStruct((depth, 2 * width), BF16),
        grid_spec=pltpu.PrefetchScalarGridSpec(
            num_scalar_prefetch=1,
            grid=(1,),
            in_specs=[whole, whole, pl.BlockSpec((None, depth, 2 * depth), lambda i, c: (0, 0, 0))],
            out_specs=pl.BlockSpec((depth, 2 * width), lambda i, c: (0, 0)),
            scratch_shapes=[pltpu.VMEM((depth, width), F32), pltpu.VMEM((depth, 2 * width), BF16)],
        ),
        cost_estimate=pl.CostEstimate(flops=2 * depth * depth * width * 3, bytes_accessed=4 * depth * depth, transcendentals=0),
        name="first_weights",
    )(core, mine, other, factors)


def update(panel_ref, split, current_ref, out_ref):
    panel = panel_ref[...].reshape(split.shape[0], panel_ref.shape[2])
    wide = lax.dot_general(panel, split[...], (((0,), (0,)), ((), ())), preferred_element_type=F32)
    out_ref[...] = current_ref[...] - fold(wide)


def apply_kernel(weights_ref, panel_ref, current_ref, out_ref):
    update(panel_ref, weights_ref, current_ref, out_ref)


STEPS = 4


def apply_first(weights, panels, current):
    sources, _, own, n_rows = panels.shape
    depth, width = weights.shape[0], current.shape[1]
    block = n_rows // STEPS
    rows = pl.BlockSpec((block, width), lambda i: (i, 0))
    return pl.pallas_call(
        apply_kernel,
        out_shape=jax.ShapeDtypeStruct(current.shape, F32),
        grid=(STEPS,),
        in_specs=[
            pl.BlockSpec(weights.shape, lambda i: (0, 0)),
            pl.BlockSpec((sources, None, own, block), lambda i: (0, 0, 0, i)),
            rows,
        ],
        out_specs=rows,
        cost_estimate=pl.CostEstimate(
            flops=2 * n_rows * depth * width * 2, bytes_accessed=panels.size + current.size * 8, transcendentals=0
        ),
        name="apply_first",
    )(weights, panels, current)


def finish_kernel(
    first_row, core_ref, mine_ref, other_ref, factor_ref, own_part, other_part, panel_ref, current_ref, out_ref, total, split
):
    @pl.when(pl.program_id(0) == 0)
    def _():
        corrections = (own_part, other_part)
        store_pieces(split, weigh(first_row, core_ref, mine_ref, other_ref, factor_ref, total, split, corrections))

    update(panel_ref, split, current_ref, out_ref)


def finish(core, mine, other, factors, own_part, other_part, panels, current, first_row):
    sources, _, own, n_rows = panels.shape
    depth, width = own_part.shape
    block = n_rows // STEPS
    whole = lambda array: pl.BlockSpec(array.shape, lambda i, c: (0, 0))
    rows = pl.BlockSpec((block, width), lambda i, c: (i, 0))
    flops = 2 * n_rows * depth * width * 2 + 2 * depth * depth * width * 3
    return pl.pallas_call(
        functools.partial(finish_kernel, first_row),
        out_shape=jax.ShapeDtypeStruct(current.shape, F32),
        grid_spec=pltpu.PrefetchScalarGridSpec(
            num_scalar_prefetch=1,
            grid=(STEPS,),
            in_specs=[
                whole(mine),
                whole(other),
                pl.BlockSpec((None, depth, 2 * depth), lambda i, c: (1, 0, 0)),
                whole(own_part),
                whole(other_part),
                pl.BlockSpec((sources, None, own, block), lambda i, c: (0, 1, 0, i)),
                rows,
            ],
            out_specs=rows,
            scratch_shapes=[pltpu.VMEM((depth, width), F32), pltpu.VMEM((depth, 2 * width), BF16)],
        ),
        cost_estimate=pl.CostEstimate(flops=flops, bytes_accessed=panels.size + current.size * 8, transcendentals=0),
        name="finish",
    )(core, mine, other, factors, own_part, other_part, panels, current)


def couple_kernel(core_ref, gram_ref, weights_ref, after_ref, out_ref):
    del after_ref
    sources, rows, width = gram_ref.shape
    half = weights_ref.shape[0] // 2
    tiles = half // width
    own = rows // tiles
    result = None
    for t in range(tiles):
        gram = gram_ref[:, own * t : own * (t + 1)].reshape(sources * own, width)
        high = gram.astype(BF16)
        low = (gram - high.astype(F32)).astype(BF16)
        start = pl.multiple_of(core_ref[0] * half + width * t, width)
        term = in_pieces(high, low, weights_ref[pl.ds(start, width)])
        result = term if result is None else result + term
    out_ref[...] = result


def couple(core, gram, weights, after):
    depth, width = weights.shape[0], weights.shape[1] // 2
    return pl.pallas_call(
        couple_kernel,
        out_shape=jax.ShapeDtypeStruct((depth, width), F32),
        in_specs=[
            pl.BlockSpec(memory_space=pltpu.SMEM),
            pl.BlockSpec(memory_space=pltpu.VMEM),
            pl.BlockSpec(memory_space=pltpu.VMEM),
            pl.BlockSpec(memory_space=pl.ANY),
        ],
        out_specs=pl.BlockSpec(memory_space=pltpu.VMEM),
        cost_estimate=pl.CostEstimate(flops=depth * depth * width * 3, bytes_accessed=gram.size * 4, transcendentals=0),
        name="couple",
    )(core, gram, weights, after)


def on_device(vectors, band_head, band_tail, band_factor, panel_vectors, panel_factor):
    margin = band_tail.shape[1]
    width = vectors.shape[1]
    depth = panel_factor.shape[1]
    core_index = lax.axis_index("row") % 2
    even = core_index == 0
    core = core_index.astype(jnp.int32).reshape(1)
    n = lax.axis_size("row")
    near_groups, far_groups = row_groups(n)

    panel_copies = copies(panel_vectors, lax.axis_size("vec"))
    panels = exchanged(panel_copies, "vec")

    factors = prepare(panel_factor)
    factor = jnp.triu(band_factor[0])
    own = product(band_head, vectors)
    tail = product(band_tail, vectors[:margin])
    cross = product_nt(band_tail, band_head[:, :margin])
    tail_next = lax.ppermute(tail, "row", [(i + 1, i) for i in range(0, n, 2)])
    weights_a = product(factor, own + tail_next)
    weights_a_prev = lax.ppermute(weights_a, "row", [(i, i + 1) for i in range(0, n, 2)])
    tail_b = tail - product(cross, weights_a)
    tail_b_next = lax.ppermute(tail_b, "row", [(i, (i - 1) % n) for i in range(0, n, 2)])
    weights_b = product(factor, own - product_t(cross, weights_a_prev) + tail_b_next)
    weights_b_prev = lax.ppermute(weights_b, "row", [(i, (i + 1) % n) for i in range(1, n, 2)])
    weights_own = jnp.where(even, weights_a, weights_b)
    weights_prev = jnp.where(even, weights_b_prev, weights_a_prev)
    current = vectors - product_t(band_head, weights_own)
    top = current[:margin] - product_t(band_tail, weights_prev)
    current = jnp.concatenate([top, current[margin:]], axis=0)

    send, keep = project(core, panels, panel_vectors, current, factors)
    blocks = (keep + swapped(send)).reshape(len(near_groups[0]), -1, width)
    share = jnp.sum(exchanged(blocks, "row", near_groups), axis=0)
    share = jnp.sum(to_everyone(share, "row", far_groups), axis=0)
    mine = to_everyone(share, "row", near_groups).reshape(-1, width)
    half = depth // 2
    gram_end = mine.shape[0] - half
    gram = to_everyone(mine[half:gram_end], "vec")
    other = swapped(mine)

    weights0 = first_weights(core, mine, other, factors)
    current = apply_first(weights0, panels, current)
    coupled = couple(core, gram, weights0, current)
    return finish(core, mine, other, factors, coupled, swapped(coupled), panels, current, gram_end)


def solution(mesh):
    return jax.shard_map(
        on_device,
        mesh=mesh,
        in_specs=(
            P("row", "vec"),
            P(None, "row"),
            P(None, "row"),
            P("row", None, None),
            P(None, "vec", "row"),
            P(),
        ),
        out_specs=P("row", "vec"),
        check_vma=False,
    )
```

time: 222 us -> 216 us (0.973)
  blocking collectives: 103 us -> 93.9 us
  starting transfers between devices: 56.6 us -> 59.7 us
    all_to_all x3, blocking collectives: 103 us -> 93.9 us  [exchanged(): lax.all_to_all(blocks, axis, split_axis=0, concat_axis=0, tiled=True, axi...]
    ppermute x7, starting transfers between devices: 44.5 us -> 48.1 us  [the longest x3 31.2 us: swapped(): lax.ppermute(array, 'row', [(i, i ^ 1) for i in range(lax.axis_size('row'...]
    pallas_call x1 -> x2, Pallas kernels: 2.41 us -> 4.95 us  [the longest x1 2.76 us: prepare(): pl.pallas_call(prepare_kernel, out_shape=jax.ShapeDtypeStruct((count, dep...]
  transfers between devices with their start and end apart: 9 -> 9, of which waited for: 5 -> 6; matrix products, arithmetic and copies ran while one was open for 3% -> 3% of each run, Pallas kernels for 3% -> 5%
where the time goes in v4:
time: 216 us; the launch traced here: 215 us
  blocking collectives  93.9 us (43%)
  starting transfers between devices  59.7 us (28%)
  Pallas kernels  26.7 us (12%)
  waiting for transfers between devices  24.3 us (11%)
  matrix products  5.29 us (2%)
  local copies, waits for them, and re-layouts  3.29 us (2%)
    all_to_all x3, blocking collectives, exchanged(): lax.all_to_all(blocks, axis, split_axis=0, concat_axis=0, tiled=True, axi...  93.9 us
    ppermute x3, starting transfers between devices, swapped(): lax.ppermute(array, 'row', [(i, i ^ 1) for i in range(lax.axis_size('row'...  31.2 us
    all_to_all x2, waiting for transfers between devices, exchanged(): lax.all_to_all(blocks, axis, split_axis=0, concat_axis=0, tiled=True, axi...  15 us
    ppermute x1, starting transfers between devices, on_device(): tail_next = lax.ppermute(tail, 'row', [(i + 1, i) for i in range(0, n, 2)])  12.9 us
    all_to_all x2, starting transfers between devices, exchanged(): lax.all_to_all(blocks, axis, split_axis=0, concat_axis=0, tiled=True, axi...  11.7 us
    pallas_call x1, Pallas kernels, project(): pl.pallas_call(project_kernel, out_shape=[jax.ShapeDtypeStruct((total, wi...  5.98 us
    pallas_call x1, Pallas kernels, finish(): pl.pallas_call(functools.partial(finish_kernel, first_row), out_shape=jax...  5.54 us
    ppermute x1, waiting for transfers between devices, on_device(): lax.ppermute(weights_a, 'row', [(i, i + 1) for i in range(0, n, 2)])  4.76 us
  transfers between devices with their start and end apart: 9, of which 6 were waited for; matrix products, arithmetic and copies ran while one was open for 3% of the time, Pallas kernels for 5%

profile of v4, /device:TPU:1, one launch (start us, length us, event | category | flops | bytes accessed | tf_op | source)
XLA Modules:
  0.0 215.5 jit_solution(16463201047235118969)
XLA Ops:
  0.0 3.1 %copies.1 = bf16[16,2,32,2048]{3,2,1,0:T(8,128)(2,1)} custom-call(bf16[2,32,2048]{2,1,0:T(8,128)(2,1)} %own_ref.1), custom_call_target="tpu_custom_call" | custom-call | tf_op jit(solution)/shard_map/copies/pallas_call | solution.py:72
  3.2 7.8 %all-to-all-start = ((bf16[16,2,32,2048]{3,2,1,0:T(8,128)(2,1)}), bf16[16,2,32,2048]{3,2,1,0:T(8,128)(2,1)}, u32[]{:S(2)}, u32[]{:S(2)}) async-start(bf16[16,2,32,2048]{3,2,1,0:T(8,128)(2,1)} %copies.1), calls=%async_computation | async-start | bytes 8388608 | tf_op jit(solution)/shard_map/all_to_all | solution.py:41
  11.3 12.9 %collective-permute-start = (f32[128,128]{1,0:T(8,128)S(1)}, f32[128,128]{1,0:T(8,128)S(1)}, u32[]{:S(2)}, u32[]{:S(2)}) collective-permute-start(f32[128,128]{1,0:T(8,128)S(1)} %fusion.5), channel_id=1, source_target_pairs={{16,0},{48,32},{80,64},{112,96},{144,128},{176,160},{208,192},{240... | collective-permute-start | bytes 196616 | tf_op jit(solution)/shard_map/ppermute | solution.py:332
  26.3 1.3 collective-permute-start.2
  27.6 1.3 collective-permute-start.1
  28.9 2.8 %prepare.1.after_ref.factor_ref = bf16[2,512,1024]{2,1,0:T(8,128)(2,1)} custom-call(f32[2,512,512]{2,1,0:T(8,128)} %factor_ref.1), custom_call_target="tpu_custom_call" | custom-call | flops 524288 | bytes 4194304 | tf_op jit(solution)/shard_map/prepare/pallas_call | solution.py:148
  32.3 4.8 %collective-permute-done.1 = f32[128,128]{1,0:T(8,128)S(1)} collective-permute-done((f32[128,128]{1,0:T(8,128)S(1)}, f32[128,128]{1,0:T(8,128)S(1)}, u32[]{:S(2)}, u32[]{:S(2)}) %collective-permute-start.1) | collective-permute-done | bytes 65568 | tf_op jit(solution)/shard_map/ppermute | solution.py:334
  37.6 1.3 collective-permute-start.3
  38.9 1.8 fusion
  42.5 15.0 %all-to-all-done.panel_ref = bf16[16,2,32,2048]{3,2,1,0:T(8,128)(2,1)} async-done(((bf16[16,2,32,2048]{3,2,1,0:T(8,128)(2,1)}), bf16[16,2,32,2048]{3,2,1,0:T(8,128)(2,1)}, u32[]{:S(2)}, u32[]{:S(2)}) %all-to-all-start) | async-done | bytes 4194336 | tf_op jit(solution)/shard_map/all_to_all | solution.py:41
  57.4 6.0 %project.1 = (f32[576,128]{1,0:T(8,128)}, f32[576,128]{1,0:T(8,128)}) custom-call(s32[1]{0:T(128)} %bitcast.core_ref, bf16[16,2,32,2048]{3,2,1,0:T(8,128)(2,1)} %all-to-all-done.panel_ref, bf16[2,32,2048]{2,1,0:T(8,128)(2,1)} %own_ref.1, f32[2048,128]{1,0:T(8,128)} %pad_maximum_fusion.current_ref, bf16[2,512,1024]{2,1,0:T(8,128)(2,1)} %prepare.1.after_ref.factor_ref), custom_call_target="tpu_custom_call" | custom-call | flops 1073741824 | bytes 5242880 | tf_op jit(solution)/shard_map/project/pallas_call | solution.py:116
  63.4 13.5 %collective-permute-start.4 = (f32[576,128]{1,0:T(8,128)}, f32[576,128]{1,0:T(8,128)S(1)}, u32[]{:S(2)}, u32[]{:S(2)}) collective-permute-start(f32[576,128]{1,0:T(8,128)} %get-tuple-element.8), channel_id=1, source_target_pairs={{0,16},{16,0},{32,48},{48,32},{64,80},{80,64},{96,112},{112,96},{1... | collective-permute-start | bytes 884744 | tf_op jit(solution)/shard_map/ppermute | solution.py:50
  76.9 1.4 collective-permute-done.4
  79.3 36.1 %all_to_all.25 = f32[8,72,128]{2,1,0:T(8,128)S(1)} all-to-all(f32[8,72,128]{2,1,0:T(8,128)S(1)} %bitcast.30), channel_id=1, replica_groups={{0,32,64,96,128,160,192,224},{256,288,320,352,384,416,448,480},{512,544..., dimensions={0} | all-to-all | bytes 589824 | tf_op jit(solution)/shard_map/all_to_all | solution.py:41
  115.5 33.3 %all_to_all.26 = f32[4,72,128]{2,1,0:T(8,128)S(1)} all-to-all(f32[4,72,128]{2,1,0:T(8,128)S(1)} %broadcast_in_dim.14), channel_id=1, replica_groups={{0,256,512,768},{32,288,544,800},{64,320,576,832},{96,352,608,864},{128..., dimensions={0} | all-to-all | bytes 294912 | tf_op jit(solution)/shard_map/all_to_all | solution.py:41
  148.8 24.5 %all_to_all.27 = f32[8,72,128]{2,1,0:T(8,128)S(1)} all-to-all(f32[8,72,128]{2,1,0:T(8,128)S(1)} %broadcast_in_dim.15), channel_id=1, replica_groups={{0,32,64,96,128,160,192,224},{256,288,320,352,384,416,448,480},{512,544..., dimensions={0} | all-to-all | bytes 589824 | tf_op jit(solution)/shard_map/all_to_all | solution.py:41
  174.3 3.9 %all-to-all-start.4 = ((f32[16,64,128]{2,1,0:T(8,128)}), f32[16,64,128]{2,1,0:T(8,128)S(1)}, u32[]{:S(2)}, u32[]{:S(2)}) async-start(f32[16,64,128]{2,1,0:T(8,128)} %broadcast_in_dim.16), calls=%async_computation.4 | async-start | bytes 1048576 | tf_op jit(solution)/shard_map/all_to_all | solution.py:41
  178.2 15.4 %collective-permute-start.5 = (f32[576,128]{1,0:T(8,128)S(1)}, f32[576,128]{1,0:T(8,128)S(1)}, u32[]{:S(2)}, u32[]{:S(2)}) collective-permute-start(f32[576,128]{1,0:T(8,128)S(1)} %bitcast.27), channel_id=1, source_target_pairs={{0,16},{16,0},{32,48},{48,32},{64,80},{80,64},{96,112},{112,96},{1... | collective-permute-start | bytes 884744 | tf_op jit(solution)/shard_map/ppermute | solution.py:50
  195.5 2.6 %first_weights.1.weights_ref = bf16[512,256]{1,0:T(8,128)(2,1)} custom-call(s32[1]{0:T(128)} %bitcast.core_ref, f32[576,128]{1,0:T(8,128)} %bitcast.28, f32[576,128]{1,0:T(8,128)} %copy-done.5, bf16[2,512,1024]{2,1,0:T(8,128)(2,1)} %prepare.1.after_ref.factor_ref), custom_call_target="tpu_custom_call" | custom-call | flops 201326592 | bytes 1048576 | tf_op jit(solution)/shard_map/first_weights/pallas_call | solution.py:189
  198.1 4.5 %apply_first.1.after_ref.current_ref = f32[2048,128]{1,0:T(8,128)} custom-call(bf16[512,256]{1,0:T(8,128)(2,1)} %first_weights.1.weights_ref, bf16[16,2,32,2048]{3,2,1,0:T(8,128)(2,1)} %all-to-all-done.panel_ref, f32[2048,128]{1,0:T(8,128)} %pad_maximum_fusion.current_ref), custom_call_target="tpu_custom_call" | custom-call | flops 536870912 | bytes 4194304 | tf_op jit(solution)/shard_map/apply_first/pallas_call | solution.py:222
  203.4 2.2 %couple.1.own_part = f32[512,128]{1,0:T(8,128)} custom-call(s32[1]{0:T(128)} %bitcast.core_ref, f32[16,64,128]{2,1,0:T(8,128)} %copy-done.4, bf16[512,256]{1,0:T(8,128)(2,1)} %first_weights.1.weights_ref, f32[2048,128]{1,0:T(8,128)} %apply_first.1.after_ref.current_ref), custom_call_target="tpu_custom_call" | custom-call | flops 100663296 | bytes 524288 | tf_op jit(solution)/shard_map/couple/pallas_call | solution.py:299
  205.6 2.3 %collective-permute-start.6 = (f32[512,128]{1,0:T(8,128)}, f32[512,128]{1,0:T(8,128)S(1)}, u32[]{:S(2)}, u32[]{:S(2)}) collective-permute-start(f32[512,128]{1,0:T(8,128)} %couple.1.own_part), channel_id=1, source_target_pairs={{0,16},{16,0},{32,48},{48,32},{64,80},{80,64},{96,112},{112,96},{1... | collective-permute-start | bytes 786440 | tf_op jit(solution)/shard_map/ppermute | solution.py:50
  207.9 1.4 collective-permute-done.6.other_part
  209.9 5.5 %finish.1 = f32[2048,128]{1,0:T(8,128)} custom-call(s32[1]{0:T(128)} %bitcast.core_ref, f32[576,128]{1,0:T(8,128)} %bitcast.29, f32[576,128]{1,0:T(8,128)} %copy-done.5, bf16[2,512,1024]{2,1,0:T(8,128)(2,1)} %prepare.1.after_ref.factor_ref, f32[512,128]{1,0:T(8,128)} %couple.1.own_part, f32[512,128]{1,0:T(8,128)} %copy-done.6, ...), custom_call_target="tpu_custom_call" | custom-call | flops 738197504 | bytes 4194304 | tf_op jit(solution)/shard_map/finish/pallas_call | solution.py:257
  (39 shorter events, 10.7 us)
Async XLA Ops:
  0.0 10.9 %copy-start = (f32[128,512]{1,0:T(8,128)S(1)}, f32[128,512]{1,0:T(8,128)}, u32[]{:S(2)}) copy-start(f32[128,512]{1,0:T(8,128)} %param.8) | copy-start | bytes 786436
  3.1 7.8 %copy-start.1 = (f32[2048,128]{1,0:T(8,128)S(1)}, f32[2048,128]{1,0:T(8,128)}, u32[]{:S(2)}) copy-start(f32[2048,128]{1,0:T(8,128)} %param.6) | copy-start | bytes 3145732
  3.1 21.2 %copy-start.2 = (f32[128,2048]{1,0:T(8,128)S(1)}, f32[128,2048]{1,0:T(8,128)}, u32[]{:S(2)}) copy-start(f32[128,2048]{1,0:T(8,128)} %param.7) | copy-start | bytes 3145732
  3.1 22.7 %copy-start.7 = (f32[1,128,128]{2,1,0:T(8,128)S(1)}, f32[1,128,128]{2,1,0:T(8,128)}, u32[]{:S(2)}) copy-start(f32[1,128,128]{2,1,0:T(8,128)} %param.9) | copy-start | bytes 196612
  3.2 54.3 %all-to-all-start = ((bf16[16,2,32,2048]{3,2,1,0:T(8,128)(2,1)}), bf16[16,2,32,2048]{3,2,1,0:T(8,128)(2,1)}, u32[]{:S(2)}, u32[]{:S(2)}) async-start(bf16[16,2,32,2048]{3,2,1,0:T(8,128)(2,1)} %copies.1), calls=%async_computation | async-start | bytes 8388608 | tf_op jit(solution)/shard_map/all_to_all | solution.py:41
  11.3 14.5 %collective-permute-start = (f32[128,128]{1,0:T(8,128)S(1)}, f32[128,128]{1,0:T(8,128)S(1)}, u32[]{:S(2)}, u32[]{:S(2)}) collective-permute-start(f32[128,128]{1,0:T(8,128)S(1)} %fusion.5), channel_id=1, source_target_pairs={{16,0},{48,32},{80,64},{112,96},{144,128},{176,160},{208,192},{240... | collective-permute-start | bytes 196616 | tf_op jit(solution)/shard_map/ppermute | solution.py:332
  26.3 6.0 %collective-permute-start.2 = (f32[128,128]{1,0:T(8,128)S(1)}, f32[128,128]{1,0:T(8,128)S(1)}, u32[]{:S(2)}, u32[]{:S(2)}) collective-permute-start(f32[128,128]{1,0:T(8,128)S(1)} %convolution_subtract_fusion), channel_id=1, source_target_pairs={{0,1008},{32,16},{64,48},{96,80},{128,112},{160,144},{192,176},{22... | collective-permute-start | bytes 196616 | tf_op jit(solution)/shard_map/ppermute | solution.py:336
  27.6 9.4 %collective-permute-start.1 = (f32[128,128]{1,0:T(8,128)S(1)}, f32[128,128]{1,0:T(8,128)S(1)}, u32[]{:S(2)}, u32[]{:S(2)}) collective-permute-start(f32[128,128]{1,0:T(8,128)S(1)} %fusion.9), channel_id=1, source_target_pairs={{0,16},{32,48},{64,80},{96,112},{128,144},{160,176},{192,208},{224... | collective-permute-start | bytes 196616 | tf_op jit(solution)/shard_map/ppermute | solution.py:334
  37.6 3.2 %collective-permute-start.3 = (f32[128,128]{1,0:T(8,128)S(1)}, f32[128,128]{1,0:T(8,128)S(1)}, u32[]{:S(2)}, u32[]{:S(2)}) collective-permute-start(f32[128,128]{1,0:T(8,128)S(1)} %fusion.11), channel_id=1, source_target_pairs={{16,32},{48,64},{80,96},{112,128},{144,160},{176,192},{208,224},{2... | collective-permute-start | bytes 196616 | tf_op jit(solution)/shard_map/ppermute | solution.py:338
  63.4 14.9 %collective-permute-start.4 = (f32[576,128]{1,0:T(8,128)}, f32[576,128]{1,0:T(8,128)S(1)}, u32[]{:S(2)}, u32[]{:S(2)}) collective-permute-start(f32[576,128]{1,0:T(8,128)} %get-tuple-element.8), channel_id=1, source_target_pairs={{0,16},{16,0},{32,48},{48,32},{64,80},{80,64},{96,112},{112,96},{1... | collective-permute-start | bytes 884744 | tf_op jit(solution)/shard_map/ppermute | solution.py:50
  173.3 21.5 %copy-start.3 = (f32[8,72,128]{2,1,0:T(8,128)}, f32[8,72,128]{2,1,0:T(8,128)S(1)}, u32[]{:S(2)}) copy-start(f32[8,72,128]{2,1,0:T(8,128)S(1)} %all_to_all.27) | copy-start | bytes 884740
  174.3 28.3 %all-to-all-start.4 = ((f32[16,64,128]{2,1,0:T(8,128)}), f32[16,64,128]{2,1,0:T(8,128)S(1)}, u32[]{:S(2)}, u32[]{:S(2)}) async-start(f32[16,64,128]{2,1,0:T(8,128)} %broadcast_in_dim.16), calls=%async_computation.4 | async-start | bytes 1048576 | tf_op jit(solution)/shard_map/all_to_all | solution.py:41
  178.2 16.6 %collective-permute-start.5 = (f32[576,128]{1,0:T(8,128)S(1)}, f32[576,128]{1,0:T(8,128)S(1)}, u32[]{:S(2)}, u32[]{:S(2)}) collective-permute-start(f32[576,128]{1,0:T(8,128)S(1)} %bitcast.27), channel_id=1, source_target_pairs={{0,16},{16,0},{32,48},{48,32},{64,80},{80,64},{96,112},{112,96},{1... | collective-permute-start | bytes 884744 | tf_op jit(solution)/shard_map/ppermute | solution.py:50
  194.8 0.7 copy-start.5
  202.6 0.8 copy-start.4
  205.6 3.6 %collective-permute-start.6 = (f32[512,128]{1,0:T(8,128)}, f32[512,128]{1,0:T(8,128)S(1)}, u32[]{:S(2)}, u32[]{:S(2)}) collective-permute-start(f32[512,128]{1,0:T(8,128)} %couple.1.own_part), channel_id=1, source_target_pairs={{0,16},{16,0},{32,48},{48,32},{64,80},{80,64},{96,112},{112,96},{1... | collective-permute-start | bytes 786440 | tf_op jit(solution)/shard_map/ppermute | solution.py:50
  209.2 0.7 copy-start.6

commit v5 on v4

--- a/solution.py
+++ b/solution.py
@@ -60,26 +60,30 @@
     return near_groups, far_groups
 
 
-def copies_kernel(source_ref, out_ref, sems):
-    moves = [pltpu.make_async_copy(source_ref, out_ref.at[i], sems.at[i]) for i in range(out_ref.shape[0])]
+def copies_kernel(index, source_ref, *refs):
+    out_ref, sems = refs[-2:]
+    moves = [
+        pltpu.make_async_copy(source_ref.at[index], out_ref.at[i], sems.at[i]) for i in range(out_ref.shape[0])
+    ]
     for move in moves:
         move.start()
     for move in moves:
         move.wait()
 
 
-def copies(array, count):
-    return pl.pallas_call(
-        copies_kernel,
-        out_shape=jax.ShapeDtypeStruct((count, *array.shape), array.dtype),
-        in_specs=[pl.BlockSpec(memory_space=pltpu.VMEM)],
+def copies(array, index, count, after=()):
+    return pl.pallas_call(
+        functools.partial(copies_kernel, index),
+        out_shape=jax.ShapeDtypeStruct((count, *array.shape[1:]), array.dtype),
+        in_specs=[pl.BlockSpec(memory_space=pltpu.VMEM)] + [pl.BlockSpec(memory_space=pl.ANY)] * len(after),
         out_specs=pl.BlockSpec(memory_space=pl.ANY),
         scratch_shapes=[pltpu.SemaphoreType.DMA((count,))],
+        compiler_params=pltpu.CompilerParams(vmem_limit_bytes=8 << 20 if after else None),
         name="copies",
-    )(array)
-
-
-def project_kernel(core_ref, panel_ref, own_ref, current_ref, after_ref, send_ref, keep_ref, split):
+    )(array, *after)
+
+
+def project_kernel(core_ref, panel0_ref, panel1_ref, own_ref, current_ref, after_ref, send_ref, keep_ref, split):
     del core_ref, after_ref
     step = pl.program_id(0)
 
@@ -87,43 +91,40 @@
     def _():
         store_pieces(split, current_ref[...])
 
-    rows = panel_ref.shape[0] * panel_ref.shape[1]
+    rows = panel0_ref.shape[0] * panel0_ref.shape[1]
     own, width = own_ref.shape[0], current_ref.shape[1]
     tiles = rows // width
-    gram_end = rows + own * tiles
-    panel = panel_ref[...].reshape(rows, panel_ref.shape[2])
-    part = fold(jnp.dot(panel, split[...], preferred_element_type=F32))
+    panel0 = panel0_ref[...].reshape(rows, panel0_ref.shape[2])
+    panel1 = panel1_ref[...].reshape(rows, panel1_ref.shape[2])
+    part0 = fold(jnp.dot(panel0, split[...], preferred_element_type=F32))
+    part1 = fold(jnp.dot(panel1, split[...], preferred_element_type=F32))
+    gram = lax.dot_general(own_ref[...], panel0, (((1,), (1,)), ((), ())), preferred_element_type=F32)
     for which, out_ref in enumerate((send_ref, keep_ref)):
 
-        @pl.when(step == 2 * which)
+        @pl.when(step == which)
         def _(out_ref=out_ref):
-            out_ref[:rows] = part
-            gram = lax.dot_general(own_ref[...], panel, (((1,), (1,)), ((), ())), preferred_element_type=F32)
+            out_ref[:rows] = part0
             for t in range(tiles):
                 out_ref[rows + own * t : rows + own * (t + 1)] = gram[:, width * t : width * (t + 1)]
-
-        @pl.when(step == 2 * which + 1)
-        def _(out_ref=out_ref):
-            out_ref[gram_end:] = part
-
-
-def project(core, panels, panel_vectors, current, after):
-    sources, _, own, depth_rows = panels.shape
+            out_ref[rows + own * tiles :] = part1
+
+
+def project(core, panel0, panel1, panel_vectors, current, after):
+    sources, own, depth_rows = panel0.shape
     rows, width = sources // 2 * own, current.shape[1]
     total = 2 * rows + own * (rows // width)
     whole = pl.BlockSpec((total, width), lambda i, c: (0, 0))
+    half = pl.BlockSpec((sources // 2, own, depth_rows), lambda i, c: (jnp.where(i == 0, 1 - c[0], c[0]), 0, 0))
     flops = 2 * 2 * sources * own * depth_rows * width * 2
     return pl.pallas_call(
         project_kernel,
         out_shape=[jax.ShapeDtypeStruct((total, width), F32)] * 2,
         grid_spec=pltpu.PrefetchScalarGridSpec(
             num_scalar_prefetch=1,
-            grid=(4,),
+            grid=(2,),
             in_specs=[
-                pl.BlockSpec(
-                    (sources // 2, None, own, depth_rows),
-                    lambda i, c: (jnp.where(i < 2, 1 - c[0], c[0]), i % 2, 0, 0),
-                ),
+                half,
+                half,
                 pl.BlockSpec((None, own, depth_rows), lambda i, c: (1, 0, 0)),
                 pl.BlockSpec(current.shape, lambda i, c: (0, 0)),
                 pl.BlockSpec(memory_space=pl.ANY),
@@ -131,9 +132,10 @@
             out_specs=[whole, whole],
             scratch_shapes=[pltpu.VMEM((depth_rows, 2 * width), BF16)],
         ),
-        cost_estimate=pl.CostEstimate(flops=flops, bytes_accessed=panels.size * 2 + current.size * 4, transcendentals=0),
+        compiler_params=pltpu.CompilerParams(vmem_limit_bytes=24 << 20),
+        cost_estimate=pl.CostEstimate(flops=flops, bytes_accessed=panel0.size * 4 + current.size * 4, transcendentals=0),
         name="project",
-    )(core, panels, panel_vectors, current, after)
+    )(core, panel0, panel1, panel_vectors, current, after)
 
 
 def prepare_kernel(factor_ref, out_ref):
@@ -214,8 +216,8 @@
 STEPS = 4
 
 
-def apply_first(weights, panels, current):
-    sources, _, own, n_rows = panels.shape
+def apply_first(weights, panel, current):
+    sources, own, n_rows = panel.shape
     depth, width = weights.shape[0], current.shape[1]
     block = n_rows // STEPS
     rows = pl.BlockSpec((block, width), lambda i: (i, 0))
@@ -225,15 +227,15 @@
         grid=(STEPS,),
         in_specs=[
             pl.BlockSpec(weights.shape, lambda i: (0, 0)),
-            pl.BlockSpec((sources, None, own, block), lambda i: (0, 0, 0, i)),
+            pl.BlockSpec((sources, own, block), lambda i: (0, 0, i)),
             rows,
         ],
         out_specs=rows,
         cost_estimate=pl.CostEstimate(
-            flops=2 * n_rows * depth * width * 2, bytes_accessed=panels.size + current.size * 8, transcendentals=0
+            flops=2 * n_rows * depth * width * 2, bytes_accessed=panel.size * 2 + current.size * 8, transcendentals=0
         ),
         name="apply_first",
-    )(weights, panels, current)
+    )(weights, panel, current)
 
 
 def finish_kernel(
@@ -247,8 +249,8 @@
     update(panel_ref, split, current_ref, out_ref)
 
 
-def finish(core, mine, other, factors, own_part, other_part, panels, current, first_row):
-    sources, _, own, n_rows = panels.shape
+def finish(core, mine, other, factors, own_part, other_part, panel, current, first_row):
+    sources, own, n_rows = panel.shape
     depth, width = own_part.shape
     block = n_rows // STEPS
     whole = lambda array: pl.BlockSpec(array.shape, lambda i, c: (0, 0))
@@ -266,15 +268,15 @@
                 pl.BlockSpec((None, depth, 2 * depth), lambda i, c: (1, 0, 0)),
                 whole(own_part),
                 whole(other_part),
-                pl.BlockSpec((sources, None, own, block), lambda i, c: (0, 1, 0, i)),
+                pl.BlockSpec((sources, own, block), lambda i, c: (0, 0, i)),
                 rows,
             ],
             out_specs=rows,
             scratch_shapes=[pltpu.VMEM((depth, width), F32), pltpu.VMEM((depth, 2 * width), BF16)],
         ),
-        cost_estimate=pl.CostEstimate(flops=flops, bytes_accessed=panels.size + current.size * 8, transcendentals=0),
+        cost_estimate=pl.CostEstimate(flops=flops, bytes_accessed=panel.size * 2 + current.size * 8, transcendentals=0),
         name="finish",
-    )(core, mine, other, factors, own_part, other_part, panels, current)
+    )(core, mine, other, factors, own_part, other_part, panel, current)
 
 
 def couple_kernel(core_ref, gram_ref, weights_ref, after_ref, out_ref):
@@ -321,8 +323,9 @@
     n = lax.axis_size("row")
     near_groups, far_groups = row_groups(n)
 
-    panel_copies = copies(panel_vectors, lax.axis_size("vec"))
-    panels = exchanged(panel_copies, "vec")
+    vec = lax.axis_size("vec")
+    vectors, panel0_copies = lax.optimization_barrier((vectors, copies(panel_vectors, 0, vec)))
+    panel0 = exchanged(panel0_copies, "vec")
 
     factors = prepare(panel_factor)
     factor = jnp.triu(band_factor[0])
@@ -342,7 +345,8 @@
     top = current[:margin] - product_t(band_tail, weights_prev)
     current = jnp.concatenate([top, current[margin:]], axis=0)
 
-    send, keep = project(core, panels, panel_vectors, current, factors)
+    panel1 = exchanged(copies(panel_vectors, 1, vec, (current, factors)), "vec")
+    send, keep = project(core, panel0, panel1, panel_vectors, current, factors)
     blocks = (keep + swapped(send)).reshape(len(near_groups[0]), -1, width)
     share = jnp.sum(exchanged(blocks, "row", near_groups), axis=0)
     share = jnp.sum(to_everyone(share, "row", far_groups), axis=0)
@@ -353,9 +357,9 @@
     other = swapped(mine)
 
     weights0 = first_weights(core, mine, other, factors)
-    current = apply_first(weights0, panels, current)
+    current = apply_first(weights0, panel0, current)
     coupled = couple(core, gram, weights0, current)
-    return finish(core, mine, other, factors, coupled, swapped(coupled), panels, current, gram_end)
+    return finish(core, mine, other, factors, coupled, swapped(coupled), panel1, current, gram_end)
 
 
 def solution(mesh):

time: 216 us -> 212 us (0.981)
  blocking collectives: 93.9 us -> 110 us
  waiting for transfers between devices: 24.3 us -> 9.24 us
  starting transfers between devices: 59.7 us -> 52.9 us
  local copies, waits for them, and re-layouts: 3.29 us -> 5.46 us
    all_to_all x3 -> x4, blocking collectives: 93.9 us -> 110 us  [exchanged(): lax.all_to_all(blocks, axis, split_axis=0, concat_axis=0, tiled=True, axi...]
    all_to_all x2, waiting for transfers between devices: 15 us -> 0.01 us  [exchanged(): lax.all_to_all(blocks, axis, split_axis=0, concat_axis=0, tiled=True, axi...]
    ppermute x3, starting transfers between devices: 31.2 us -> 24.8 us  [swapped(): lax.ppermute(array, 'row', [(i, i ^ 1) for i in range(lax.axis_size('row'...]
    unnamed x16 -> x28, local copies, waits for them, and re-layouts: 2.26 us -> 4.45 us
    pallas_call x1 -> x2, Pallas kernels: 3.1 us -> 5.3 us  [copies(): pl.pallas_call(functools.partial(copies_kernel, index), out_shape=jax.Sha...]
  transfers between devices with their start and end apart: 9 -> 9, of which waited for: 6 -> 5; matrix products, arithmetic and copies ran while one was open for 3% -> 3% of each run, Pallas kernels for 5% -> 6%
where the time goes in v5:
time: 212 us; the launch traced here: 211 us
  blocking collectives  110 us (52%)
  starting transfers between devices  52.9 us (25%)
  Pallas kernels  27.1 us (13%)
  waiting for transfers between devices  9.24 us (4%)
  matrix products  6.36 us (3%)
  local copies, waits for them, and re-layouts  5.46 us (3%)
    all_to_all x4, blocking collectives, exchanged(): lax.all_to_all(blocks, axis, split_axis=0, concat_axis=0, tiled=True, axi...  110 us
    ppermute x3, starting transfers between devices, swapped(): lax.ppermute(array, 'row', [(i, i ^ 1) for i in range(lax.axis_size('row'...  24.8 us
    ppermute x1, starting transfers between devices, on_device(): tail_next = lax.ppermute(tail, 'row', [(i + 1, i) for i in range(0, n, 2)])  12.8 us
    all_to_all x2, starting transfers between devices, exchanged(): lax.all_to_all(blocks, axis, split_axis=0, concat_axis=0, tiled=True, axi...  11.3 us
    pallas_call x1, Pallas kernels, finish(): pl.pallas_call(functools.partial(finish_kernel, first_row), out_shape=jax...  5.55 us
    pallas_call x2, Pallas kernels, copies(): pl.pallas_call(functools.partial(copies_kernel, index), out_shape=jax.Sha...  5.3 us
    ppermute x1, waiting for transfers between devices, on_device(): lax.ppermute(weights_a, 'row', [(i, i + 1) for i in range(0, n, 2)])  4.86 us
    pallas_call x1, Pallas kernels, apply_first(): pl.pallas_call(apply_kernel, out_shape=jax.ShapeDtypeStruct(current.shape...  4.65 us
  transfers between devices with their start and end apart: 9, of which 5 were waited for; matrix products, arithmetic and copies ran while one was open for 3% of the time, Pallas kernels for 6%

profile of v5, /device:TPU:1, one launch (start us, length us, event | category | flops | bytes accessed | tf_op | source)
XLA Modules:
  0.0 211.1 jit_solution(12436551239803925340)
XLA Ops:
  0.0 2.4 %copies.2 = bf16[16,32,2048]{2,1,0:T(8,128)(2,1)} custom-call(bf16[2,32,2048]{2,1,0:T(8,128)(2,1)} %own_ref.1), custom_call_target="tpu_custom_call" | custom-call | tf_op jit(solution)/shard_map/copies/pallas_call | solution.py:75
  2.5 7.8 %all-to-all-start = ((bf16[16,32,2048]{2,1,0:T(8,128)(2,1)}), bf16[16,32,2048]{2,1,0:T(8,128)(2,1)}, u32[]{:S(2)}, u32[]{:S(2)}) async-start(bf16[16,32,2048]{2,1,0:T(8,128)(2,1)} %copies.2), calls=%async_computation | async-start | bytes 4194304 | tf_op jit(solution)/shard_map/all_to_all | solution.py:41
  10.9 12.8 %collective-permute-start = (f32[128,128]{0,1:T(8,128)S(1)}, f32[128,128]{0,1:T(8,128)S(1)}, u32[]{:S(2)}, u32[]{:S(2)}) collective-permute-start(f32[128,128]{0,1:T(8,128)S(1)} %convolution_bitcast_fusion.3), channel_id=1, source_target_pairs={{16,0},{48,32},{80,64},{112,96},{144,128},{176,160},{208,192},{240... | collective-permute-start | bytes 196616 | tf_op jit(solution)/shard_map/ppermute | solution.py:335
  23.7 1.8 convolution_bitcast_fusion.2
  26.6 1.3 collective-permute-start.2
  29.2 2.7 %prepare.1.refs_1_.after_ref.factor_ref = bf16[2,512,1024]{2,1,0:T(8,128)(2,1)} custom-call(f32[2,512,512]{2,1,0:T(8,128)} %factor_ref.1), custom_call_target="tpu_custom_call" | custom-call | flops 524288 | bytes 4194304 | tf_op jit(solution)/shard_map/prepare/pallas_call | solution.py:150
  32.6 4.9 %collective-permute-done.1 = f32[128,128]{1,0:T(8,128)S(1)} collective-permute-done((f32[128,128]{1,0:T(8,128)S(1)}, f32[128,128]{1,0:T(8,128)S(1)}, u32[]{:S(2)}, u32[]{:S(2)}) %collective-permute-start.1) | collective-permute-done | bytes 65568 | tf_op jit(solution)/shard_map/ppermute | solution.py:337
  39.3 1.8 fusion
  42.7 2.9 %copies.3 = bf16[16,32,2048]{2,1,0:T(8,128)(2,1)S(1)} custom-call(bf16[2,32,2048]{2,1,0:T(8,128)(2,1)S(1)} %copy-done.5, f32[2048,128]{1,0:T(8,128)S(1)} %pad_maximum_fusion.refs_0_.current_ref, bf16[2,512,1024]{2,1,0:T(8,128)(2,1)S(1)} %copy-done.1), custom_call_target="tpu_custom_call" | custom-call | tf_op jit(solution)/shard_map/copies/pallas_call | solution.py:75
  45.6 1.3 copy-done.4
  47.0 31.1 %all_to_all.30.panel1_ref.panel_ref = bf16[16,32,2048]{2,1,0:T(8,128)(2,1)S(1)} all-to-all(bf16[16,32,2048]{2,1,0:T(8,128)(2,1)} %copy-done.4), channel_id=1, replica_groups=mesh['row'=64,'vec'=16] {'vec'}, dimensions={0} | all-to-all | bytes 4194304 | tf_op jit(solution)/shard_map/all_to_all | solution.py:41
  78.1 4.1 %project.1 = (f32[576,128]{1,0:T(8,128)S(1)}, f32[576,128]{1,0:T(8,128)S(1)}) custom-call(s32[1]{0:T(128)} %bitcast.core_ref, bf16[16,32,2048]{2,1,0:T(8,128)(2,1)} %all-to-all-done.panel0_ref.panel_ref, bf16[16,32,2048]{2,1,0:T(8,128)(2,1)S(1)} %all_to_all.30.panel1_ref.panel_ref, bf16[2,32,2048]{2,1,0:T(8,128)(2,1)S(1)} %copy-done.6, ...), custom_call_target="tpu_custom_call" | custom-call | flops 1073741824 | bytes 5242880 | tf_op jit(solution)/shard_map/project/pallas_call | solution.py:119
  82.2 7.9 %collective-permute-start.4 = (f32[576,128]{1,0:T(8,128)S(1)}, f32[576,128]{1,0:T(8,128)S(1)}, u32[]{:S(2)}, u32[]{:S(2)}) collective-permute-start(f32[576,128]{1,0:T(8,128)S(1)} %get-tuple-element.12), channel_id=1, source_target_pairs={{0,16},{16,0},{32,48},{48,32},{64,80},{80,64},{96,112},{112,96},{1... | collective-permute-start | bytes 884744 | tf_op jit(solution)/shard_map/ppermute | solution.py:50
  91.3 20.6 %all_to_all.31 = f32[8,72,128]{2,1,0:T(8,128)S(1)} all-to-all(f32[8,72,128]{2,1,0:T(8,128)S(1)} %bitcast.34), channel_id=1, replica_groups={{0,32,64,96,128,160,192,224},{256,288,320,352,384,416,448,480},{512,544..., dimensions={0} | all-to-all | bytes 589824 | tf_op jit(solution)/shard_map/all_to_all | solution.py:41
  111.9 33.3 %all_to_all.32 = f32[4,72,128]{2,1,0:T(8,128)S(1)} all-to-all(f32[4,72,128]{2,1,0:T(8,128)S(1)} %broadcast_in_dim.14), channel_id=1, replica_groups={{0,256,512,768},{32,288,544,800},{64,320,576,832},{96,352,608,864},{128..., dimensions={0} | all-to-all | bytes 294912 | tf_op jit(solution)/shard_map/all_to_all | solution.py:41
  145.3 24.5 %all_to_all.33 = f32[8,72,128]{2,1,0:T(8,128)S(1)} all-to-all(f32[8,72,128]{2,1,0:T(8,128)S(1)} %broadcast_in_dim.15), channel_id=1, replica_groups={{0,32,64,96,128,160,192,224},{256,288,320,352,384,416,448,480},{512,544..., dimensions={0} | all-to-all | bytes 589824 | tf_op jit(solution)/shard_map/all_to_all | solution.py:41
  170.7 3.6 %all-to-all-start.5 = ((f32[16,64,128]{2,1,0:T(8,128)}), f32[16,64,128]{2,1,0:T(8,128)S(1)}, u32[]{:S(2)}, u32[]{:S(2)}) async-start(f32[16,64,128]{2,1,0:T(8,128)} %broadcast_in_dim.16), calls=%async_computation.5 | async-start | bytes 1048576 | tf_op jit(solution)/shard_map/all_to_all | solution.py:41
  174.3 14.7 %collective-permute-start.5 = (f32[576,128]{1,0:T(8,128)S(1)}, f32[576,128]{1,0:T(8,128)S(1)}, u32[]{:S(2)}, u32[]{:S(2)}) collective-permute-start(f32[576,128]{1,0:T(8,128)S(1)} %bitcast.31), channel_id=1, source_target_pairs={{0,16},{16,0},{32,48},{48,32},{64,80},{80,64},{96,112},{112,96},{1... | collective-permute-start | bytes 884744 | tf_op jit(solution)/shard_map/ppermute | solution.py:50
  191.0 2.6 %first_weights.1.weights_ref = bf16[512,256]{1,0:T(8,128)(2,1)} custom-call(s32[1]{0:T(128)} %bitcast.core_ref, f32[576,128]{1,0:T(8,128)} %bitcast.32, f32[576,128]{1,0:T(8,128)} %copy-done.11, bf16[2,512,1024]{2,1,0:T(8,128)(2,1)} %prepare.1.refs_1_.after_ref.factor_ref), custom_call_target="tpu_custom_call" | custom-call | flops 201326592 | bytes 1048576 | tf_op jit(solution)/shard_map/first_weights/pallas_call | solution.py:191
  193.6 4.7 %apply_first.1.after_ref.current_ref = f32[2048,128]{1,0:T(8,128)} custom-call(bf16[512,256]{1,0:T(8,128)(2,1)} %first_weights.1.weights_ref, bf16[16,32,2048]{2,1,0:T(8,128)(2,1)} %all-to-all-done.panel0_ref.panel_ref, f32[2048,128]{1,0:T(8,128)} %copy-done.3), custom_call_target="tpu_custom_call" | custom-call | flops 536870912 | bytes 4194304 | tf_op jit(solution)/shard_map/apply_first/pallas_call | solution.py:224
  199.0 2.2 %couple.1.own_part = f32[512,128]{1,0:T(8,128)} custom-call(s32[1]{0:T(128)} %bitcast.core_ref, f32[16,64,128]{2,1,0:T(8,128)} %copy-done.10, bf16[512,256]{1,0:T(8,128)(2,1)} %first_weights.1.weights_ref, f32[2048,128]{1,0:T(8,128)} %apply_first.1.after_ref.current_ref), custom_call_target="tpu_custom_call" | custom-call | flops 100663296 | bytes 524288 | tf_op jit(solution)/shard_map/couple/pallas_call | solution.py:301
  201.2 2.3 %collective-permute-start.6 = (f32[512,128]{1,0:T(8,128)}, f32[512,128]{1,0:T(8,128)S(1)}, u32[]{:S(2)}, u32[]{:S(2)}) collective-permute-start(f32[512,128]{1,0:T(8,128)} %couple.1.own_part), channel_id=1, source_target_pairs={{0,16},{16,0},{32,48},{48,32},{64,80},{80,64},{96,112},{112,96},{1... | collective-permute-start | bytes 786440 | tf_op jit(solution)/shard_map/ppermute | solution.py:50
  203.5 1.4 collective-permute-done.6.other_part
  205.5 5.5 %finish.1 = f32[2048,128]{1,0:T(8,128)} custom-call(s32[1]{0:T(128)} %bitcast.core_ref, f32[576,128]{1,0:T(8,128)} %bitcast.33, f32[576,128]{1,0:T(8,128)} %copy-done.11, bf16[2,512,1024]{2,1,0:T(8,128)(2,1)} %prepare.1.refs_1_.after_ref.factor_ref, f32[512,128]{1,0:T(8,128)} %couple.1.own_part, f32[512,128]{1,0:T(8,128)} %copy-done.13, ...), custom_call_target="tpu_custom_call" | custom-call | flops 738197504 | bytes 4194304 | tf_op jit(solution)/shard_map/finish/pallas_call | solution.py:259
  (53 shorter events, 12.6 us)
Async XLA Ops:
  0.0 10.3 %copy-start = (f32[128,512]{1,0:T(8,128)S(1)}, f32[128,512]{1,0:T(8,128)}, u32[]{:S(2)}) copy-start(f32[128,512]{1,0:T(8,128)} %param.8) | copy-start | bytes 786436
  2.5 7.8 %copy-start.7 = (f32[2048,128]{1,0:T(8,128)S(1)}, f32[2048,128]{1,0:T(8,128)}, u32[]{:S(2)}) copy-start(f32[2048,128]{1,0:T(8,128)} %param.6) | copy-start | bytes 3145732
  2.5 21.3 %copy-start.8 = (f32[128,2048]{1,0:T(8,128)S(1)}, f32[128,2048]{1,0:T(8,128)}, u32[]{:S(2)}) copy-start(f32[128,2048]{1,0:T(8,128)} %param.7) | copy-start | bytes 3145732
  2.5 44.5 %all-to-all-start = ((bf16[16,32,2048]{2,1,0:T(8,128)(2,1)}), bf16[16,32,2048]{2,1,0:T(8,128)(2,1)}, u32[]{:S(2)}, u32[]{:S(2)}) async-start(bf16[16,32,2048]{2,1,0:T(8,128)(2,1)} %copies.2), calls=%async_computation | async-start | bytes 4194304 | tf_op jit(solution)/shard_map/all_to_all | solution.py:41
  10.3 15.7 %copy-start.12 = (f32[1,128,128]{2,1,0:T(8,128)S(1)}, f32[1,128,128]{2,1,0:T(8,128)}, u32[]{:S(2)}) copy-start(f32[1,128,128]{2,1,0:T(8,128)} %param.9) | copy-start | bytes 196612
  10.9 15.1 %collective-permute-start = (f32[128,128]{0,1:T(8,128)S(1)}, f32[128,128]{0,1:T(8,128)S(1)}, u32[]{:S(2)}, u32[]{:S(2)}) collective-permute-start(f32[128,128]{0,1:T(8,128)S(1)} %convolution_bitcast_fusion.3), channel_id=1, source_target_pairs={{16,0},{48,32},{80,64},{112,96},{144,128},{176,160},{208,192},{240... | collective-permute-start | bytes 196616 | tf_op jit(solution)/shard_map/ppermute | solution.py:335
  26.6 6.0 %collective-permute-start.2 = (f32[128,128]{0,1:T(8,128)S(1)}, f32[128,128]{0,1:T(8,128)S(1)}, u32[]{:S(2)}, u32[]{:S(2)}) collective-permute-start(f32[128,128]{0,1:T(8,128)S(1)} %convolution_subtract_fusion), channel_id=1, source_target_pairs={{0,1008},{32,16},{64,48},{96,80},{128,112},{160,144},{192,176},{22... | collective-permute-start | bytes 196616 | tf_op jit(solution)/shard_map/ppermute | solution.py:339
  27.9 9.5 %collective-permute-start.1 = (f32[128,128]{1,0:T(8,128)S(1)}, f32[128,128]{1,0:T(8,128)S(1)}, u32[]{:S(2)}, u32[]{:S(2)}) collective-permute-start(f32[128,128]{1,0:T(8,128)S(1)} %fusion.8), channel_id=1, source_target_pairs={{0,16},{32,48},{64,80},{96,112},{128,144},{160,176},{192,208},{224... | collective-permute-start | bytes 196616 | tf_op jit(solution)/shard_map/ppermute | solution.py:337
  38.0 3.2 %collective-permute-start.3 = (f32[128,128]{1,0:T(8,128)S(1)}, f32[128,128]{1,0:T(8,128)S(1)}, u32[]{:S(2)}, u32[]{:S(2)}) collective-permute-start(f32[128,128]{1,0:T(8,128)S(1)} %fusion.10), channel_id=1, source_target_pairs={{16,32},{48,64},{80,96},{112,128},{144,160},{176,192},{208,224},{2... | collective-permute-start | bytes 196616 | tf_op jit(solution)/shard_map/ppermute | solution.py:341
  41.1 1.6 copy-start.1
  41.1 1.6 copy-start.5
  42.7 35.4 %copy-start.3 = (f32[2048,128]{1,0:T(8,128)}, f32[2048,128]{1,0:T(8,128)S(1)}, u32[]{:S(2)}) copy-start(f32[2048,128]{1,0:T(8,128)S(1)} %pad_maximum_fusion.refs_0_.current_ref) | copy-start | bytes 3145732
  45.6 1.4 copy-start.4
  46.9 31.1 %copy-start.6 = (bf16[2,32,2048]{2,1,0:T(8,128)(2,1)S(1)}, bf16[2,32,2048]{2,1,0:T(8,128)(2,1)}, u32[]{:S(2)}) copy-start(bf16[2,32,2048]{2,1,0:T(8,128)(2,1)} %own_ref.1) | copy-start | bytes 786436
  78.1 4.1 %copy-start.2 = (bf16[16,32,2048]{2,1,0:T(8,128)(2,1)}, bf16[16,32,2048]{2,1,0:T(8,128)(2,1)S(1)}, u32[]{:S(2)}) copy-start(bf16[16,32,2048]{2,1,0:T(8,128)(2,1)S(1)} %all_to_all.30.panel1_ref.panel_ref) | copy-start | bytes 6291460
  82.2 9.1 %collective-permute-start.4 = (f32[576,128]{1,0:T(8,128)S(1)}, f32[576,128]{1,0:T(8,128)S(1)}, u32[]{:S(2)}, u32[]{:S(2)}) collective-permute-start(f32[576,128]{1,0:T(8,128)S(1)} %get-tuple-element.12), channel_id=1, source_target_pairs={{0,16},{16,0},{32,48},{48,32},{64,80},{80,64},{96,112},{112,96},{1... | collective-permute-start | bytes 884744 | tf_op jit(solution)/shard_map/ppermute | solution.py:50
  169.8 20.4 %copy-start.9 = (f32[8,72,128]{2,1,0:T(8,128)}, f32[8,72,128]{2,1,0:T(8,128)S(1)}, u32[]{:S(2)}) copy-start(f32[8,72,128]{2,1,0:T(8,128)S(1)} %all_to_all.33) | copy-start | bytes 884740
  170.7 27.5 %all-to-all-start.5 = ((f32[16,64,128]{2,1,0:T(8,128)}), f32[16,64,128]{2,1,0:T(8,128)S(1)}, u32[]{:S(2)}, u32[]{:S(2)}) async-start(f32[16,64,128]{2,1,0:T(8,128)} %broadcast_in_dim.16), calls=%async_computation.5 | async-start | bytes 1048576 | tf_op jit(solution)/shard_map/all_to_all | solution.py:41
  174.3 15.9 %collective-permute-start.5 = (f32[576,128]{1,0:T(8,128)S(1)}, f32[576,128]{1,0:T(8,128)S(1)}, u32[]{:S(2)}, u32[]{:S(2)}) collective-permute-start(f32[576,128]{1,0:T(8,128)S(1)} %bitcast.31), channel_id=1, source_target_pairs={{0,16},{16,0},{32,48},{48,32},{64,80},{80,64},{96,112},{112,96},{1... | collective-permute-start | bytes 884744 | tf_op jit(solution)/shard_map/ppermute | solution.py:50
  190.2 0.7 copy-start.11
  198.2 0.8 copy-start.10
  201.2 3.6 %collective-permute-start.6 = (f32[512,128]{1,0:T(8,128)}, f32[512,128]{1,0:T(8,128)S(1)}, u32[]{:S(2)}, u32[]{:S(2)}) collective-permute-start(f32[512,128]{1,0:T(8,128)} %couple.1.own_part), channel_id=1, source_target_pairs={{0,16},{16,0},{32,48},{48,32},{64,80},{80,64},{96,112},{112,96},{1... | collective-permute-start | bytes 786440 | tf_op jit(solution)/shard_map/ppermute | solution.py:50
  204.8 0.7 copy-start.13
